TPU v7x, 32 devices: a whole 2x2x4 slice. The times are simulated.
32 devices in a mesh: dp: 4 (over y, core), ctx: 8 (over z, x).
Axes of the slice: x: 2, y: 2, z: 4, core: 2. Of those that a mesh axis runs over, the one named last changes fastest.
Arguments:
- tokens: bfloat16 [4, 1024, 1024], P('dp', 'ctx'), may hold values from -8 to 8
- lengths: int32 [4], P('dp'), may hold values from 256 to 1024, as said below
- attn_gain: float32 [1024], replicated, may hold values from 0.25 to 1.75
- q_gain: float32 [64], replicated, may hold values from 0.25 to 1.75
- k_gain: float32 [64], replicated, may hold values from 0.25 to 1.75
- w_query: bfloat16 [1024, 1024], replicated, may hold values from -0.1875 to 0.1875
- w_key: bfloat16 [1024, 512], replicated, may hold values from -0.1875 to 0.1875
- w_value: bfloat16 [1024, 512], replicated, may hold values from -0.1875 to 0.1875
- w_out: bfloat16 [1024, 1024], replicated, may hold values from -3 to 3
- ffn_gain: float32 [1024], replicated, may hold values from 0.25 to 1.75
- w_gate: bfloat16 [1024, 4608], replicated, may hold values from -0.1875 to 0.1875
- w_up: bfloat16 [1024, 4608], replicated, may hold values from -0.1875 to 0.1875
- w_down: bfloat16 [4608, 1024], replicated, may hold values from -0.09375 to 0.09375
- cotangent: bfloat16 [4, 1024, 1024], P('dp', 'ctx'), may hold values from -8 to 8
Outputs:
- result: bfloat16 [4, 1024, 1024], P('dp', 'ctx')
- grad_tokens: float32 [4, 1024, 1024], P('dp', 'ctx')
- attn_gain_grad: float32 [1024], replicated
- q_gain_grad: float32 [64], replicated
- k_gain_grad: float32 [64], replicated
- query_grad: float32 [1024, 1024], P(('dp', 'ctx'))
- key_grad: float32 [1024, 512], P(('dp', 'ctx'))
- value_grad: float32 [1024, 512], P(('dp', 'ctx'))
- out_grad: float32 [1024, 1024], P(None, ('dp', 'ctx'))
- ffn_gain_grad: float32 [1024], replicated
- gate_grad: float32 [1024, 4608], P(('dp', 'ctx'))
- up_grad: float32 [1024, 4608], P(('dp', 'ctx'))
- down_grad: float32 [4608, 1024], P(None, ('dp', 'ctx'))
Inputs may be any that keep to these rules, and one draw needn't show every extreme that they name: `lengths`: each sequence's true length; at least one sequence fills all 1024 slots.
All inputs are finite; a program needn't handle non-finite values.
Results may differ from a plain program's by a relative error of at most 0.018.
Values may be sent and summed in bfloat16 or wider, within the bound.
No kernel may reach another device: no remote copies, remote signals or barrier semaphores. Data moves between devices by JAX's collectives and lax.ppermute only.
A program may use at most 320 MiB of HBM per device.

v0:
```python
import math

import jax
import jax.numpy as jnp
from jax import lax
from jax.experimental import pallas as pl
from jax.experimental.pallas import tpu as pltpu
from jax.sharding import PartitionSpec as P

EPS = 1e-05
THETA = 1000000.0
MASKED = -1e30


def passed_along(shard, axis, by):
    count = lax.axis_size(axis)
    pairs = [(i, i + by) for i in range(count) if 0 <= i + by < count]
    return lax.ppermute(shard, axis, pairs)


def from_behind(value, axis, steps):
    count = lax.axis_size(axis)
    pairs = [(source, (source + steps) % count) for source in range(count)]
    return lax.ppermute(value, axis, pairs)


def root_norm(values, gain):
    return values * lax.rsqrt(jnp.mean(values * values, axis=-1, keepdims=True) + EPS) * gain


def rotate(values, cosine, sine):
    half = values.shape[-1] // 2
    first_half = values[..., :half]
    second_half = values[..., half:]
    return jnp.concatenate(
        [first_half * cosine - second_half * sine, second_half * cosine + first_half * sine],
        axis=-1,
    )


def angles(positions, width):
    freqs = THETA ** (-(jnp.arange(width // 2, dtype=jnp.float32) * 2.0 / width))
    turned = positions.astype(jnp.float32)[:, None] * freqs[None, :]
    return (jnp.cos(turned), jnp.sin(turned))


def query_form(flat, gain, cosine, sine, groups):
    seq_count, row_count, width = flat.shape
    head_dim = gain.shape[0]
    normed = root_norm(flat.reshape(seq_count, row_count, width // head_dim, head_dim), gain)
    turned = rotate(normed, cosine, sine)
    return turned.reshape(seq_count, row_count, -1, groups, head_dim).transpose(0, 2, 3, 1, 4)


def key_form(flat, gain, cosine, sine):
    seq_count, row_count, width = flat.shape
    head_dim = gain.shape[0]
    normed = root_norm(flat.reshape(seq_count, row_count, width // head_dim, head_dim), gain)
    return rotate(normed, cosine, sine)


def ring_form(
    tokens,
    lengths,
    attn_gain,
    q_gain,
    k_gain,
    w_query,
    w_key,
    w_value,
    w_out,
    ffn_gain,
    w_gate,
    w_up,
    w_down,
    cotangent,
):
    seq_count, row_count, width = tokens.shape
    head_dim = q_gain.shape[0]
    heads = w_query.shape[1] // head_dim
    kv_heads = w_key.shape[1] // head_dim
    groups = heads // kv_heads
    loop_size = lax.axis_size("ctx")
    my_place = lax.axis_index("ctx")
    query_start = my_place * row_count
    query_pos = query_start + jnp.arange(row_count, dtype=jnp.int32)
    longest = jnp.max(lengths)
    cosine, sine = angles(query_pos, head_dim)
    cosine = cosine[None, :, None, :]
    sine = sine[None, :, None, :]
    inputs = tokens.astype(jnp.float32)
    acts = root_norm(inputs, attn_gain).astype(jnp.bfloat16).reshape(-1, width)
    qproj = jnp.dot(acts, w_query, preferred_element_type=jnp.float32).reshape(
        seq_count, row_count, -1
    )
    kproj = jnp.dot(acts, w_key, preferred_element_type=jnp.float32).reshape(
        seq_count, row_count, -1
    )
    vproj = jnp.dot(acts, w_value, preferred_element_type=jnp.float32)
    queries = query_form(qproj, q_gain, cosine, sine, groups).astype(jnp.bfloat16)
    keys = key_form(kproj, k_gain, cosine, sine).astype(jnp.bfloat16)
    values = vproj.astype(jnp.bfloat16).reshape(seq_count, row_count, kv_heads, head_dim)
    key_values = jnp.stack([keys, values])

    def block_mask(key_start, count):
        key_pos = key_start + jnp.arange(count, dtype=jnp.int32)
        causal = key_pos[None, None, :] <= query_pos[None, :, None]
        inside = key_pos[None, None, :] < lengths[:, None, None]
        return (causal & inside)[:, None, None, :, :]

    def needed(key_start):
        return (key_start < query_start + row_count) & (key_start < longest)

    def scores_of(key_piece):
        return 0.125 * jnp.einsum(
            "scgtd,sucd->scgtu", queries, key_piece, preferred_element_type=jnp.float32
        )

    def absorb(state, pair, key_start):

        def absorb_work(current):
            top_row, row_total, summed = current
            counted = block_mask(key_start, pair.shape[2])
            masked = jnp.where(counted, scores_of(pair[0]), MASKED)
            top_new = jnp.maximum(top_row, jnp.max(masked, axis=-1))
            weights = jnp.where(counted, jnp.exp(masked - top_new[..., None]), 0.0)
            factor = jnp.exp(top_row - top_new)
            row_total = row_total * factor + jnp.sum(weights, axis=-1)
            summed = summed * factor[..., None] + jnp.einsum(
                "scgtu,sucd->scgtd",
                weights.astype(jnp.bfloat16),
                pair[1],
                preferred_element_type=jnp.float32,
            )
            return (top_new, row_total, summed)

        return lax.cond(needed(key_start), absorb_work, lambda current: current, state)

    stat_shape = (seq_count, kv_heads, groups, row_count)
    start_state = (
        jnp.full(stat_shape, MASKED, jnp.float32),
        jnp.zeros(stat_shape, jnp.float32),
        jnp.zeros(stat_shape + (head_dim,), jnp.float32),
    )
    first_state = absorb(start_state, key_values, query_start)

    def forward_turn(step, carry):
        held, state = carry
        held = passed_along(held, "ctx", 1)
        source = (my_place - step) % loop_size
        return (held, absorb(state, held, source * row_count))

    _, (top_row, row_total, summed) = lax.fori_loop(
        1, loop_size, forward_turn, (key_values, first_state)
    )
    attended = summed / row_total[..., None]
    attn_low = attended.astype(jnp.bfloat16)
    out_heads = w_out.reshape(kv_heads, groups, head_dim, width)
    attn_branch = jnp.einsum(
        "scgtd,cgde->ste", attn_low, out_heads, preferred_element_type=jnp.float32
    )
    middle = inputs + attn_branch
    inner = root_norm(middle, ffn_gain).astype(jnp.bfloat16).reshape(-1, width)
    gate_proj = jnp.dot(inner, w_gate, preferred_element_type=jnp.float32)
    up_proj = jnp.dot(inner, w_up, preferred_element_type=jnp.float32)
    hidden = (jax.nn.silu(gate_proj) * up_proj).astype(jnp.bfloat16)
    output = middle + jnp.dot(hidden, w_down, preferred_element_type=jnp.float32).reshape(
        seq_count, row_count, width
    )
    result = output.astype(jnp.bfloat16)
    valid = (query_pos[None, :] < lengths[:, None]).astype(jnp.float32)
    grad_out = cotangent.astype(jnp.float32) * valid[..., None]
    grad_low = grad_out.astype(jnp.bfloat16).reshape(-1, width)
    down_turned = jnp.einsum("nd,nf->df", grad_low, hidden, preferred_element_type=jnp.float32)
    grad_hidden = jnp.einsum("nd,fd->nf", grad_low, w_down, preferred_element_type=jnp.float32)
    _, pull_gate = jax.vjp(lambda gate_in, up_in: jax.nn.silu(gate_in) * up_in, gate_proj, up_proj)
    grad_gate, grad_up = pull_gate(grad_hidden)
    gate_low = grad_gate.astype(jnp.bfloat16)
    up_low = grad_up.astype(jnp.bfloat16)
    gate_local = jnp.einsum("nd,nf->df", inner, gate_low, preferred_element_type=jnp.float32)
    up_local = jnp.einsum("nd,nf->df", inner, up_low, preferred_element_type=jnp.float32)
    grad_inner = jnp.einsum("nf,df->nd", gate_low, w_gate, preferred_element_type=jnp.float32)
    grad_inner = grad_inner + jnp.einsum(
        "nf,df->nd", up_low, w_up, preferred_element_type=jnp.float32
    )
    _, pull_second = jax.vjp(root_norm, middle, ffn_gain)
    grad_middle, ffn_local = pull_second(grad_inner.reshape(seq_count, row_count, width))
    grad_middle = grad_middle + grad_out
    branch_low = grad_middle.astype(jnp.bfloat16)
    out_turned = jnp.einsum(
        "std,scgte->dcge", branch_low, attn_low, preferred_element_type=jnp.float32
    ).reshape(width, -1)
    grad_attended = jnp.einsum(
        "ste,cgde->scgtd", branch_low, out_heads, preferred_element_type=jnp.float32
    ).astype(jnp.bfloat16)
    grad_wide = grad_attended.astype(jnp.float32)
    delta = jnp.sum(grad_wide * attended, axis=-1)
    grad_scaled = grad_wide / row_total[..., None]

    def block_back(pair, key_start):
        counted = block_mask(key_start, pair.shape[2])
        weights = jnp.where(counted, jnp.exp(scores_of(pair[0]) - top_row[..., None]), 0.0)
        probs = weights / row_total[..., None]
        grad_values = jnp.einsum(
            "scgtu,scgtd->sucd",
            weights.astype(jnp.bfloat16),
            grad_scaled,
            preferred_element_type=jnp.float32,
        )
        grad_probs = jnp.einsum(
            "scgtd,sucd->scgtu", grad_attended, pair[1], preferred_element_type=jnp.float32
        )
        grad_scores = (probs * (grad_probs - delta[..., None])).astype(jnp.bfloat16)
        more_queries = 0.125 * jnp.einsum(
            "scgtu,sucd->scgtd", grad_scores, pair[0], preferred_element_type=jnp.float32
        )
        grad_keys = 0.125 * jnp.einsum(
            "scgtu,scgtd->sucd", grad_scores, queries, preferred_element_type=jnp.float32
        )
        return (more_queries, jnp.stack([grad_keys, grad_values]))

    start_queries = jnp.zeros(stat_shape + (head_dim,), jnp.float32)

    def backward_turn(step, carry):
        held, held_grads, grad_queries = carry
        key_start = (my_place - step) % loop_size * row_count

        def backward_work(current):
            query_acc, pair_acc = current
            more_queries, more_pair = block_back(held, key_start)
            return (query_acc + more_queries, pair_acc + more_pair)

        grad_queries, held_grads = lax.cond(
            needed(key_start), backward_work, lambda current: current, (grad_queries, held_grads)
        )
        held = passed_along(held, "ctx", 1)
        held_grads = from_behind(held_grads.astype(jnp.bfloat16), "ctx", 1).astype(held_grads.dtype)
        return (held, held_grads, grad_queries)

    start_grads = jnp.zeros((2, seq_count, row_count, kv_heads, head_dim), jnp.float32)
    _, pair_grads, grad_queries = lax.fori_loop(
        0, loop_size, backward_turn, (key_values, start_grads, start_queries)
    )
    _, pull_query = jax.vjp(
        lambda proj_in, gain_in: query_form(proj_in, gain_in, cosine, sine, groups), qproj, q_gain
    )
    grad_qproj, q_local = pull_query(grad_queries)
    _, pull_key = jax.vjp(
        lambda proj_in, gain_in: key_form(proj_in, gain_in, cosine, sine), kproj, k_gain
    )
    grad_kproj, k_local = pull_key(pair_grads[0])
    query_low = grad_qproj.reshape(-1, heads * head_dim).astype(jnp.bfloat16)
    key_low = grad_kproj.reshape(-1, kv_heads * head_dim).astype(jnp.bfloat16)
    value_low = pair_grads[1].reshape(-1, kv_heads * head_dim).astype(jnp.bfloat16)
    query_local = jnp.einsum("nd,ne->de", acts, query_low, preferred_element_type=jnp.float32)
    key_local = jnp.einsum("nd,ne->de", acts, key_low, preferred_element_type=jnp.float32)
    value_local = jnp.einsum("nd,ne->de", acts, value_low, preferred_element_type=jnp.float32)
    grad_acts = jnp.einsum("ne,de->nd", query_low, w_query, preferred_element_type=jnp.float32)
    grad_acts = grad_acts + jnp.einsum(
        "ne,de->nd", key_low, w_key, preferred_element_type=jnp.float32
    )
    grad_acts = grad_acts + jnp.einsum(
        "ne,de->nd", value_low, w_value, preferred_element_type=jnp.float32
    )
    _, pull_first = jax.vjp(root_norm, inputs, attn_gain)
    grad_inputs, attn_local = pull_first(grad_acts.reshape(seq_count, row_count, width))
    grad_inputs = grad_inputs + grad_middle
    query_sum, key_sum, value_sum, out_sum, gate_sum, up_sum, down_sum = (
        lax.psum_scatter(query_local, ("dp", "ctx"), scatter_dimension=0, tiled=True),
        lax.psum_scatter(key_local, ("dp", "ctx"), scatter_dimension=0, tiled=True),
        lax.psum_scatter(value_local, ("dp", "ctx"), scatter_dimension=0, tiled=True),
        lax.psum_scatter(out_turned, ("dp", "ctx"), scatter_dimension=0, tiled=True),
        lax.psum_scatter(gate_local, ("dp", "ctx"), scatter_dimension=0, tiled=True),
        lax.psum_scatter(up_local, ("dp", "ctx"), scatter_dimension=0, tiled=True),
        lax.psum_scatter(down_turned, ("dp", "ctx"), scatter_dimension=0, tiled=True),
    )
    attn_sum, q_sum, k_sum, ffn_sum = lax.psum(
        (attn_local, q_local, k_local, ffn_local), ("dp", "ctx")
    )
    return (
        result,
        grad_inputs,
        attn_sum,
        q_sum,
        k_sum,
        query_sum,
        key_sum,
        value_sum,
        out_sum.T,
        ffn_sum,
        gate_sum,
        up_sum,
        down_sum.T,
    )


LANES = 128
VMEM_LIMIT = 60 << 20
NN = ((1,), (0,))
NT = ((1,), (1,))
TN = ((0,), (0,))


def bf16_dot(left, right, dims):
    return lax.dot_general(left, right, (dims, ((), ())), preferred_element_type=jnp.float32)


def inverse_root(values):
    return lax.rsqrt(jnp.mean(values * values, axis=-1, keepdims=True) + EPS)


def lane_of(shape):
    return lax.broadcasted_iota(jnp.int32, shape, len(shape) - 1)


def head_mean(values, head_dim):
    rows = lax.broadcasted_iota(jnp.int32, (LANES, LANES), 0) // head_dim
    columns = lane_of((LANES, LANES)) // head_dim
    spread = jnp.where(rows == columns, 1.0 / head_dim, 0.0).astype(jnp.bfloat16)
    return bf16_dot(values.astype(jnp.bfloat16), spread, NN)


def partner(values, head_dim):
    half = head_dim // 2
    first = lane_of(values.shape) % head_dim < half
    return jnp.where(
        first, pltpu.roll(values, LANES - half, axis=1), pltpu.roll(values, half, axis=1)
    )


def head_turn(flat, gain, cosine, sine, head_dim):
    normed = flat * lax.rsqrt(head_mean(flat * flat, head_dim) + EPS) * gain
    return normed * cosine + partner(normed, head_dim) * sine


def head_turn_back(grad, flat, gain, cosine, sine, head_dim):
    back = grad * cosine + partner(grad * sine, head_dim)
    root = lax.rsqrt(head_mean(flat * flat, head_dim) + EPS)
    scaled = gain * back
    mean = head_mean(scaled * flat, head_dim)
    return (
        root * scaled - flat * (root * root * root * mean),
        jnp.sum(back * flat * root, axis=0, keepdims=True),
    )


def turns(freq, base_ref, starts):
    base_cos, base_sin = base_ref[0], base_ref[1]
    cosines, sines = [], []
    for start in starts:
        angle = jnp.asarray(start, jnp.float32) * freq[0:1, :]
        cos, sin = jnp.cos(angle), jnp.sin(angle)
        cosines.append(base_cos * cos - base_sin * sin)
        sines.append((base_sin * cos + base_cos * sin) * freq[1:2, :])
    return jnp.concatenate(cosines, axis=0), jnp.concatenate(sines, axis=0)


def whole_spec(shape):
    return pl.BlockSpec(shape, lambda *_: (0,) * len(shape))


def cost_of(inputs, outs, flops):
    moved = sum(item.size * item.dtype.itemsize for item in (*inputs, *outs))
    return pl.CostEstimate(flops=flops, bytes_accessed=moved, transcendentals=0)


class Arriving:
    def __init__(self, sources, targets, signals, ref):
        self.copies = [pltpu.make_async_copy(*item) for item in zip(sources, targets, signals)]
        self.ref, self.shape = ref, ref.shape
        for copy in self.copies:
            copy.start()

    def ready(self):
        for copy in self.copies:
            copy.wait()
        self.copies = []
        return self.ref

    def __getitem__(self, at):
        return self.ready()[at]


class Leaving:
    def __init__(self, ref, target, signal):
        self.ref, self.target, self.signal, self.shape = ref, target, signal, ref.shape
        self.copy = None

    def __setitem__(self, at, value):
        self.ref[at] = value

    def __getitem__(self, at):
        return self.ref[at]

    def leave(self):
        if self.copy is None:
            self.copy = pltpu.make_async_copy(self.ref, self.target, self.signal)
            self.copy.start()


class Part:
    def __init__(self, array, index):
        self.array, self.index = array, index
        self.shape = array.shape if index is None else array.shape[1:]


class Stack:
    def __init__(self, arrays):
        self.parts = [item if isinstance(item, Part) else Part(item, None) for item in arrays]
        self.arrays, self.dtype = [item.array for item in self.parts], self.parts[0].array.dtype
        self.shape = (len(arrays),) + self.parts[0].shape
        self.size = len(arrays) * math.prod(self.parts[0].shape)

    def of(self, refs):
        return [ref if item.index is None else ref.at[item.index] for ref, item in zip(refs, self.parts)]


class Rows:
    def __init__(self, array, scalar, rows=0):
        self.array, self.scalar, self.rows = array, scalar, rows
        self.shape = (rows,) + array.shape[1:] if rows else array.shape[1:]
        self.dtype, self.size = array.dtype, array.size

    def of(self, ref, scalars):
        at = scalars[self.scalar]
        if not self.rows:
            return ref.at[at]
        return ref.at[pl.ds(pl.multiple_of(at * self.rows, self.rows), self.rows)]


def kernel_call(body, scalars, inputs, outs, scratch, flops, name, held=(), stacks=()):
    arrays = [item.arrays if isinstance(item, Stack) else [getattr(item, "array", item)] for item in inputs]
    count, kept = sum(map(len, arrays)), len(held)

    def run(scalars_ref, *refs):
        given, refs = refs[:count], refs[count + kept :]
        targets, refs = refs[: len(outs)], refs[len(outs) :]
        stack_refs, refs = refs[: len(stacks)], refs[len(stacks) :]
        buffers, refs = refs[: len(inputs)], refs[len(inputs) :]
        results, refs = refs[: len(outs)], refs[len(outs) :]
        signals, own = refs[0], refs[1:]
        arriving, used = [], 0
        for item, group, buffer in zip(inputs, arrays, buffers):
            sources = list(given[used : used + len(group)])
            places = [buffer.at[at] for at in range(len(group))] if isinstance(item, Stack) else [buffer]
            if isinstance(item, Rows):
                sources = [item.of(sources[0], scalars_ref)]
            if isinstance(item, Stack):
                sources = item.of(sources)
            slots = [signals.at[used + at] for at in range(len(group))]
            arriving.append(Arriving(sources, places, slots, buffer))
            used += len(group)
        leaving = [
            Leaving(result, target, signals.at[count + at])
            for at, (result, target) in enumerate(zip(results, targets))
        ]
        body(scalars_ref, *arriving, *leaving, *stack_refs, *own)
        for item in arriving:
            item.ready()
        for item in leaving:
            item.leave()
        for item in leaving:
            item.copy.wait()

    near = pl.BlockSpec(memory_space=pl.ANY)
    far = pl.BlockSpec(memory_space=pltpu.HBM)
    return pl.pallas_call(
        run,
        in_specs=[pl.BlockSpec(memory_space=pltpu.SMEM)] + [near] * count + [far] * kept,
        out_specs=[far] * (len(outs) + len(stacks)),
        out_shape=[*outs, *stacks],
        scratch_shapes=[pltpu.VMEM(item.shape, item.dtype) for item in (*inputs, *outs)]
        + [pltpu.SemaphoreType.DMA((count + len(outs),))]
        + list(scratch),
        input_output_aliases={1 + count + at: len(outs) + at for at in range(kept)},
        cost_estimate=cost_of(inputs, (*outs, *stacks), flops),
        compiler_params=pltpu.CompilerParams(vmem_limit_bytes=VMEM_LIMIT),
        name=name,
    )(scalars, *[array for group in arrays for array in group], *held)


def shape_of(shape, dtype):
    return jax.ShapeDtypeStruct(shape, dtype)


def stacked(values):
    return jnp.concatenate(
        [values[:, at : at + LANES] for at in range(0, values.shape[1], LANES)], axis=0
    )


def key_value_rows(scalars, shard_refs, wk_ref, wv_ref, gain_ref, k_gain_ref, freq, base_ref, acts, kv, head_dim):
    count, rows = len(shard_refs), shard_refs[0].shape[0]
    for at, ref in enumerate(shard_refs):
        values = ref[...].astype(jnp.float32)
        acts[at] = (values * inverse_root(values) * gain_ref[...]).astype(jnp.bfloat16)
    cosine, sine = turns(freq, base_ref, [scalars[at] * rows for at in range(count)])
    flat = acts[...].reshape(count * rows, -1)
    left = lane_of((count * rows, LANES)) < head_dim
    keys = bf16_dot(flat, wk_ref[...], NN)
    values = bf16_dot(flat, wv_ref[...], NN)
    for chunk in range(wk_ref.shape[1] // LANES):
        at = slice(chunk * LANES, (chunk + 1) * LANES)
        turned = head_turn(keys[:, at], k_gain_ref[...], cosine, sine, head_dim)
        value = values[:, at]
        for odd in range(2):
            pair = jnp.where(
                left,
                pltpu.roll(turned, head_dim, axis=1) if odd else turned,
                value if odd else pltpu.roll(value, head_dim, axis=1),
            )
            start = (2 * chunk + odd) * LANES
            kv[:, :, start : start + LANES] = pair.astype(jnp.bfloat16).reshape(count, rows, LANES)


def key_value_body(count, head_dim, scalars, *refs):
    shard_ref, wk_ref, wv_ref, gain_ref, k_gain_ref, freq_ref, base_ref = refs[:7]
    acts_out, kv_out, acts, kv, signals = refs[7:]
    shards, freq = shard_ref.ready(), freq_ref[...]
    for ref in (wk_ref, wv_ref, gain_ref, k_gain_ref, base_ref):
        ref.ready()

    def one_pair(pair, carry):
        both = pl.ds(2 * pair, 2)
        key_value_rows(
            [scalars[2 * pair], scalars[2 * pair + 1]],
            [shards.at[2 * pair], shards.at[2 * pair + 1]],
            wk_ref,
            wv_ref,
            gain_ref,
            k_gain_ref,
            freq,
            base_ref,
            acts.at[both],
            kv.at[both],
            head_dim,
        )
        return carry

    lax.fori_loop(0, count // 2, one_pair, 0)
    leaving = [
        pltpu.make_async_copy(buffer.at[at], out.at[scalars[at]], signals.at[2 * at + turn])
        for at in range(count)
        for turn, (buffer, out) in enumerate(((acts, acts_out), (kv, kv_out)))
    ]
    for copy in leaving:
        copy.start()
    for copy in leaving:
        copy.wait()


def key_value_part(scalars, shards, weights, parts, head_dim, held):
    rows, width = shards[0].shape
    kv_width = 2 * weights[0].shape[1]
    count = len(shards)
    return kernel_call(
        lambda *refs: key_value_body(count, head_dim, *refs),
        scalars,
        [Stack(shards), *weights],
        [],
        [
            pltpu.VMEM((count, rows, width), jnp.bfloat16),
            pltpu.VMEM((count, rows, kv_width), jnp.bfloat16),
            pltpu.SemaphoreType.DMA((2 * count,)),
        ],
        2 * count * rows * width * kv_width,
        "key_value_part",
        held,
        [
            shape_of((parts, rows, width), jnp.bfloat16),
            shape_of((parts, rows, kv_width), jnp.bfloat16),
        ],
    )


def attend_body(known, fresh, head_dim, scalars, *refs):
    shard_refs, refs = refs[:fresh], refs[fresh:]
    wk_ref, wv_ref, gain_ref, k_gain_ref, freq_ref, base_ref, x_ref, wq_ref, q_gain_ref = refs[:9]
    kv_refs, refs = refs[9 : 9 + known], refs[9 + known :]
    out_ref, acts_out, acts, kv, bias, turned, signals = refs
    place, length = scalars[known + fresh], scalars[known + fresh + 1]
    rows = x_ref.shape[0]
    count = (known + fresh) * rows
    chunks = wq_ref.shape[1] // LANES
    freq = freq_ref[...]
    key_value_rows(
        [scalars[known + at] for at in range(fresh)],
        shard_refs,
        wk_ref,
        wv_ref,
        gain_ref,
        k_gain_ref,
        freq,
        base_ref,
        acts,
        kv.at[pl.ds(known, fresh)],
        head_dim,
    )
    leaving = [
        pltpu.make_async_copy(acts.at[at], acts_out.at[scalars[known + at]], signals.at[at])
        for at in range(fresh)
    ]
    for copy in leaving:
        copy.start()
    values = x_ref[...].astype(jnp.float32)
    own = (values * inverse_root(values) * gain_ref[...]).astype(jnp.bfloat16)
    tables = turns(freq, base_ref, [place * rows])
    cosine, sine = (jnp.concatenate([table] * chunks, axis=0) for table in tables)
    flat = stacked(bf16_dot(own, wq_ref[...], NN))
    turned[...] = (0.125 * head_turn(flat, q_gain_ref[...], cosine, sine, head_dim)).reshape(
        chunks, rows, LANES
    )
    query_pos = place * rows + lane_of((rows, 2 * rows)) % rows
    for slot in range(known + fresh):
        key_pos = scalars[slot] * rows + lax.broadcasted_iota(jnp.int32, (rows, 2 * rows), 0)
        bias[slot * rows : (slot + 1) * rows, :] = jnp.where(
            (key_pos <= query_pos) & (key_pos < length), 0.0, MASKED
        )
        if slot < known:
            kv[slot] = kv_refs[slot][...]
    left = lane_of((rows, LANES)) < head_dim

    def one_head(index, carry):
        at = pl.ds(pl.multiple_of(index * LANES, LANES), LANES)
        mine = turned[index]
        both = jnp.concatenate(
            [jnp.where(left, mine, 0.0), jnp.where(left, pltpu.roll(mine, head_dim, axis=1), 0.0)],
            axis=0,
        ).astype(jnp.bfloat16)
        head_kv = kv[:, :, at].reshape(count, LANES)
        scores = bf16_dot(head_kv, both, NT) + bias[...]
        top = jnp.max(scores, axis=0, keepdims=True)
        weights = jnp.exp(scores - top)
        total = jnp.sum(weights, axis=0, keepdims=True)
        summed = bf16_dot(head_kv, weights.astype(jnp.bfloat16), TN)[head_dim:] / total
        heads = jnp.concatenate([summed[:, :rows], summed[:, rows:]], axis=0)
        out_ref[:, at] = heads.T.astype(jnp.bfloat16)
        return carry

    lax.fori_loop(0, chunks, one_head, 0)
    for copy in leaving:
        copy.wait()


def attend(scalars, shards, x_own, early, weights, w_query, q_gain, head_dim):
    parts, rows, width = early[0].shape
    q_width, kv_width = w_query.shape[1], 2 * weights[0].shape[1]
    fresh = len(shards)
    known = parts - fresh
    blocks = [Rows(early[1], at) for at in range(known)]
    return kernel_call(
        lambda *refs: attend_body(known, fresh, head_dim, *refs),
        scalars,
        [*shards, *weights, x_own, w_query, q_gain, *blocks],
        [shape_of((rows, q_width), jnp.bfloat16)],
        [
            pltpu.VMEM((fresh, rows, width), jnp.bfloat16),
            pltpu.VMEM((parts, rows, kv_width), jnp.bfloat16),
            pltpu.VMEM((parts * rows, 2 * rows), jnp.float32),
            pltpu.VMEM((q_width // LANES, rows, LANES), jnp.float32),
            pltpu.SemaphoreType.DMA((fresh,)),
        ],
        2 * rows * width * (q_width + fresh * kv_width) + 4 * rows * parts * rows * q_width,
        "attend",
        [early[0]],
        [shape_of((parts, rows, width), jnp.bfloat16)],
    )


def ffn_terms(gate, up, grad_hidden):
    sig = 1.0 / (1.0 + jnp.exp(-gate))
    swish = gate * sig
    hidden = (swish * up).astype(jnp.bfloat16)
    grad_gate = (grad_hidden * up * (sig * (1.0 + gate * (1.0 - sig)))).astype(jnp.bfloat16)
    grad_up = (grad_hidden * swish).astype(jnp.bfloat16)
    return hidden, grad_gate, grad_up


def valid_rows(values, start, length):
    pos = start + lax.broadcasted_iota(jnp.int32, (values.shape[0], 1), 0)
    return jnp.where(pos < length, values.astype(jnp.float32), 0.0).astype(jnp.bfloat16)


def ffn_body(
    sums,
    first,
    last,
    scalars,
    x_ref,
    att_ref,
    cot_ref,
    w_out_ref,
    gain_ref,
    gate_ref,
    up_ref,
    down_ref,
    *refs,
):
    if not first:
        before, refs = refs[:2], refs[2:]
    outs, (mid, inner, grad_low, out_acc, inner_acc) = refs[:-5], refs[-5:]
    step = pl.program_id(0)
    gain = gain_ref[...]
    rows = x_ref.shape[0]

    @pl.when(step == 0)
    def _():
        middle = x_ref[...].astype(jnp.float32) + bf16_dot(att_ref[...], w_out_ref[...], NN)
        mid[...] = middle
        inner[...] = (middle * inverse_root(middle) * gain).astype(jnp.bfloat16)
        grad_low[...] = valid_rows(cot_ref[...], scalars[0] * rows, scalars[1])
        out_acc[...] = middle if first else before[0][...]
        inner_acc[...] = jnp.zeros_like(inner_acc) if first else before[1][...]

    gate_w, up_w, down_w = gate_ref[...], up_ref[...], down_ref[...]
    hidden, grad_gate, grad_up = ffn_terms(
        bf16_dot(inner[...], gate_w, NN),
        bf16_dot(inner[...], up_w, NN),
        bf16_dot(grad_low[...], down_w, NT),
    )
    out_acc[...] += bf16_dot(hidden, down_w, NN)
    inner_acc[...] += bf16_dot(grad_gate, gate_w, NT) + bf16_dot(grad_up, up_w, NT)

    @pl.when(step == pl.num_programs(0) - 1)
    def _():
        if not last:
            outs[0][...] = out_acc[...]
            outs[1][...] = inner_acc[...]
            return
        result_ref, grad_mid_ref, sent_ref, gain_grad_ref = outs
        result_ref[...] = out_acc[...].astype(jnp.bfloat16)
        middle = mid[...]
        grad_inner = inner_acc[...]
        root = inverse_root(middle)
        scaled = grad_inner * gain
        mean = jnp.mean(scaled * middle, axis=-1, keepdims=True)
        grad_mid = (
            grad_low[...].astype(jnp.float32) + root * scaled - middle * (root * root * root * mean)
        )
        grad_mid_ref[...] = grad_mid
        gain_grad_ref[...] = jnp.sum(grad_inner * middle * root, axis=0, keepdims=True)
        branch = grad_mid.astype(jnp.bfloat16)
        grad_att = bf16_dot(branch, w_out_ref[...], NT)
        parts = sent_ref.shape[0]
        each = grad_mid.shape[1] // (parts * sums)
        lane = lane_of((rows, LANES))
        for part in range(parts):
            head_at = slice(part * LANES, (part + 1) * LANES)
            sent_ref[part, :, :LANES] = grad_att[:, head_at].astype(jnp.bfloat16)
            picked = jnp.zeros((rows, LANES), jnp.float32)
            for block in range(sums):
                start = (block * parts + part) * each
                chunk = grad_mid[:, start // LANES * LANES : start // LANES * LANES + LANES]
                turn = (block * each - start % LANES) % LANES
                moved = pltpu.roll(chunk, turn, axis=1) if turn else chunk
                picked = jnp.where(lane // each == block, moved, picked)
            sent_ref[part, :, LANES:] = picked.astype(jnp.bfloat16)


def ffn_part(scalars, own, weights, blocks, chunk, before, last, parts, sums):
    rows, width = own[0].shape
    low, high = blocks
    w_gate, w_up, w_down = weights
    inputs = [*own, *weights, *before]
    specs = [whole_spec(item.shape) for item in own] + [
        pl.BlockSpec((width, chunk), lambda i, s: (0, i + low)),
        pl.BlockSpec((width, chunk), lambda i, s: (0, i + low)),
        pl.BlockSpec((chunk, width), lambda i, s: (i + low, 0)),
    ]
    specs += [whole_spec(item.shape) for item in before]
    outs = [shape_of((rows, width), jnp.float32)] * 2
    if last:
        outs = [
            shape_of((rows, width), jnp.bfloat16),
            shape_of((rows, width), jnp.float32),
            shape_of((parts, rows, 2 * LANES), jnp.bfloat16),
            shape_of((1, width), jnp.float32),
        ]
    return pl.pallas_call(
        lambda *refs: ffn_body(sums, not before, last, *refs),
        grid_spec=pltpu.PrefetchScalarGridSpec(
            num_scalar_prefetch=1,
            grid=(high - low,),
            in_specs=specs,
            out_specs=[whole_spec(item.shape) for item in outs],
            scratch_shapes=[
                pltpu.VMEM((rows, width), jnp.float32),
                pltpu.VMEM((rows, width), jnp.bfloat16),
                pltpu.VMEM((rows, width), jnp.bfloat16),
                pltpu.VMEM((rows, width), jnp.float32),
                pltpu.VMEM((rows, width), jnp.float32),
            ],
        ),
        out_shape=outs,
        cost_estimate=pl.CostEstimate(
            flops=12 * rows * width * chunk * (high - low),
            bytes_accessed=6 * width * chunk * (high - low),
            transcendentals=0,
        ),
        compiler_params=pltpu.CompilerParams(vmem_limit_bytes=VMEM_LIMIT),
        name="ffn_part",
    )(scalars, *inputs)


def factor_loop(count, scalars, refs, inner_ref, grad_ref, gate_ref, up_ref, hidden_ref):
    x_ref, att_ref, cot_ref, w_out_ref, gain_ref, gate_up_ref, down_ref = refs
    x_all, att_all, cot_all = x_ref.ready(), att_ref.ready(), cot_ref.ready()
    w_out, gain, gate_up, down = w_out_ref[...], gain_ref[...], gate_up_ref[...], down_ref[...]
    rows, padded = x_ref.shape[1], down_ref.shape[0]

    def one_pair(pair, carry):
        at = pl.ds(pl.multiple_of(2 * pair * rows, 2 * rows), 2 * rows)
        both = pl.ds(2 * pair, 2)
        middle = x_all[both].reshape(2 * rows, -1).astype(jnp.float32)
        middle = middle + bf16_dot(att_all[both].reshape(2 * rows, -1), w_out, NN)
        inner = (middle * inverse_root(middle) * gain).astype(jnp.bfloat16)
        grad_low = jnp.concatenate(
            [
                valid_rows(cot_all[2 * pair + odd], scalars[2 * pair + odd] * rows, scalars[count])
                for odd in range(2)
            ],
            axis=0,
        )
        wide = bf16_dot(inner, gate_up, NN)
        grad_hidden = bf16_dot(grad_low, down, NT)
        hidden, grad_gate, grad_up = ffn_terms(wide[:, :padded], wide[:, padded:], grad_hidden)
        inner_ref[at, :], grad_ref[at, :], hidden_ref[at, :] = inner, grad_low, hidden
        gate_ref[at, :], up_ref[at, :] = grad_gate, grad_up
        return carry

    lax.fori_loop(0, count // 2, one_pair, 0)


def factor_body(count, scalars, *refs):
    factor_loop(count, scalars, refs[:7], *[ref.ref for ref in refs[7:]])


def factor_part(scalars, x_shards, att_shards, cot_shards, weights):
    rows, width = x_shards[0].shape
    columns = weights[-1].shape[0]
    count = len(x_shards)
    outs = [shape_of((count * rows, width), jnp.bfloat16)] * 2
    outs += [shape_of((count * rows, columns), jnp.bfloat16)] * 3
    return kernel_call(
        lambda *refs: factor_body(count, *refs),
        scalars,
        [Stack(x_shards), Stack(att_shards), Stack(cot_shards), *weights],
        outs,
        [],
        2 * count * rows * width * (width + 3 * columns),
        "factor_part",
    )


def cut_copies(whole, kept_out, given_out, core, signals):
    size = whole.shape[0] // 4
    copies = []
    for index, (out, bit) in enumerate(((kept_out, core), (given_out, 1 - core))):
        for half in range(2):
            start = pl.multiple_of((2 * half + bit) * size, size)
            copies.append(
                pltpu.make_async_copy(
                    whole.at[pl.ds(start, size)],
                    out.at[pl.ds(half * size, size)],
                    signals.at[2 * index + half],
                )
            )
    for copy in copies:
        copy.start()
    return copies


def last_body(count, known, columns, scalars, *refs):
    left_ref, right_ref, kept_out, given_out, lefts, rights, found, whole, signals = refs[7:]
    core = scalars[count + 1]
    factor_loop(
        count, scalars, refs[:7], lefts.at[0], lefts.at[1], rights.at[0], rights.at[1], rights.at[2]
    )
    lefts_known, rights_known = left_ref.ready(), right_ref.ready()

    def product(index, carry):
        side = index // 2
        total = bf16_dot(rights[index], lefts[side], TN)
        for at in range(known):
            total = total + bf16_dot(rights_known[index * known + at], lefts_known[side * known + at], TN)
        found[index] = total.T.astype(jnp.bfloat16)
        return carry

    lax.fori_loop(0, 3, product, 0)
    for index in range(3):
        whole[:, index * columns : (index + 1) * columns] = found[index, :, :columns]
    for copy in cut_copies(whole, kept_out, given_out, core, signals):
        copy.wait()


def last_products(scalars, x_shards, att_shards, cot_shards, weights, before, columns):
    rows, width = x_shards[0].shape
    padded = weights[-1].shape[0]
    count = len(x_shards)
    total = 3 * columns + -3 * columns % LANES
    return kernel_call(
        lambda *refs: last_body(count, len(before), columns, *refs),
        scalars,
        [
            Stack(x_shards),
            Stack(att_shards),
            Stack(cot_shards),
            *weights,
            Stack([item[side] for side in (0, 1) for item in before]),
            Stack([item[side] for side in (2, 3, 4) for item in before]),
        ],
        [],
        [
            pltpu.VMEM((2, count * rows, width), jnp.bfloat16),
            pltpu.VMEM((3, count * rows, padded), jnp.bfloat16),
            pltpu.VMEM((3, width, padded), jnp.bfloat16),
            pltpu.VMEM((width, total), jnp.bfloat16),
            pltpu.SemaphoreType.DMA((4,)),
        ],
        2 * count * rows * width * (width + 3 * padded) + 12 * count * rows * width * columns,
        "last_products",
        (),
        [shape_of((width // 2, total), jnp.bfloat16)] * 2,
    )


def head_body(head_dim, scalars, *refs):
    w_ref, q_gain_ref, k_gain_ref, freq_ref, base_ref, acts_ref, came_ref, low_ref, gains_ref = refs[:9]
    flat_q, flat_kv, cosines, sines, queries, keys, values, query_grad, key_grad, value_grad = refs[9:]
    parts, rows, width = acts_ref.shape
    count = parts * rows
    length = scalars[1]
    span = 2 * rows
    blocks = count // span
    q_gain, k_gain, freq, w = q_gain_ref[...], k_gain_ref[...], freq_ref[...], w_ref[...]
    acts, base = acts_ref.ready(), base_ref.ready()
    left = lane_of((span, LANES)) < head_dim

    def rows_of(block):
        return pl.ds(pl.multiple_of(block * span, span), span)

    def project(block, carry):
        at = rows_of(block)
        cosine, sine = turns(freq, base, [block * span, block * span + rows])
        flat = bf16_dot(acts[pl.ds(2 * block, 2)].reshape(span, width), w, NN)
        query, kv = flat[:, :LANES], flat[:, LANES:]
        flat_q[at, :], flat_kv[at, :], cosines[at, :], sines[at, :] = query, kv, cosine, sine
        queries[at, :] = (0.125 * head_turn(query, q_gain, cosine, sine, head_dim)).astype(jnp.bfloat16)
        turned = head_turn(kv, k_gain, cosine, sine, head_dim)
        keys[at, :] = jnp.where(left, turned, pltpu.roll(turned, head_dim, axis=1)).astype(jnp.bfloat16)
        values[at, :] = jnp.where(left, pltpu.roll(kv, head_dim, axis=1), kv).astype(jnp.bfloat16)
        key_grad[at, :] = jnp.zeros((span, LANES), jnp.float32)
        value_grad[at, :] = jnp.zeros((span, LANES), jnp.float32)
        return carry

    lax.fori_loop(0, blocks, project, 0)
    came = came_ref.ready()
    nothing = jnp.zeros((span, LANES), jnp.bfloat16)
    for block in range(blocks):
        extent = (block + 1) * span
        at = slice(block * span, extent)
        query_grad[...] = jnp.zeros_like(query_grad)

        def one_head(head, carry, extent=extent, at=at, block=block):
            key_pos = lax.broadcasted_iota(jnp.int32, (extent, span), 0)
            query_pos = block * span + lane_of((extent, span))
            counted = (key_pos <= query_pos) & (key_pos < length)
            mine = (lane_of((span, LANES)) // head_dim) == head
            query = jnp.where(mine, queries[at, :], nothing)
            grad = jnp.where(mine, came[2 * block : 2 * block + 2, :, :LANES].reshape(span, LANES), nothing)
            scores = jnp.where(counted, bf16_dot(keys[:extent, :], query, NT), MASKED)
            top = jnp.max(scores, axis=0, keepdims=True)
            weights = jnp.exp(scores - top)
            probs = weights * (1.0 / jnp.sum(weights, axis=0, keepdims=True))
            grad_probs = bf16_dot(values[:extent, :], grad, NT)
            delta = jnp.sum(probs * grad_probs, axis=0, keepdims=True)
            grad_scores = (probs * (grad_probs - delta)).astype(jnp.bfloat16)
            value_grad[:extent, :] += bf16_dot(probs.astype(jnp.bfloat16), grad, NN)
            key_grad[:extent, :] += bf16_dot(grad_scores, query, NN)
            own = (lane_of((extent, LANES)) // head_dim) == head
            key = jnp.where(own, keys[:extent, :], jnp.zeros((extent, LANES), jnp.bfloat16))
            query_grad[...] += bf16_dot(key, grad_scores, TN)
            return carry

        lax.fori_loop(0, 2, one_head, 0, unroll=2)
        sines_at, cosines_at = sines[at, :], cosines[at, :]
        low, q_part = head_turn_back(
            0.125 * query_grad[...].T, flat_q[at, :], q_gain, cosines_at, sines_at, head_dim
        )
        low_ref[2 * block : 2 * block + 2, :, :LANES] = low.astype(jnp.bfloat16).reshape(2, rows, LANES)
        gains_ref[0:1, :] = q_part if block == 0 else gains_ref[0:1, :] + q_part

    def finish(block, total):
        at = rows_of(block)
        key, value = key_grad[at, :], value_grad[at, :]
        key = key + pltpu.roll(key, head_dim, axis=1)
        value = value + pltpu.roll(value, head_dim, axis=1)
        low, part = head_turn_back(key, flat_kv[at, :], k_gain, cosines[at, :], sines[at, :], head_dim)
        both = jnp.where(left, low, value).astype(jnp.bfloat16).reshape(2, rows, LANES)
        low_ref.ref[pl.ds(2 * block, 2), :, LANES:] = both
        return total + part

    gains_ref[1:2, :] = lax.fori_loop(0, blocks, finish, jnp.zeros((1, LANES), jnp.float32))


def head_gradients(scalars, acts, w_head, q_gain, k_gain, freq, base, came, head_dim):
    parts, rows, width = acts.shape
    count = parts * rows
    return kernel_call(
        lambda *refs: head_body(head_dim, *refs),
        scalars,
        [w_head, q_gain, k_gain, freq, base, acts, came],
        [
            shape_of((parts, rows, 2 * LANES), jnp.bfloat16),
            shape_of((8, LANES), jnp.float32),
        ],
        [pltpu.VMEM((count, LANES), jnp.float32)] * 4
        + [pltpu.VMEM((count, LANES), jnp.bfloat16)] * 3
        + [pltpu.VMEM((LANES, 2 * rows), jnp.float32)]
        + [pltpu.VMEM((count, LANES), jnp.float32)] * 2,
        4 * count * width * LANES + 14 * count * count * head_dim,
        "head_gradients",
    )


def token_grad_body(head_dim, *refs):
    back_ref, wq_ref, wk_ref, wv_ref, x_ref, grad_mid_ref, gain_ref, out_ref = refs
    parts = back_ref.shape[0]
    back = back_ref.ready()
    left = lane_of((back.shape[1], LANES)) < head_dim
    keys, values = [], []
    for part in range(0, parts, 2):
        even = back[part, :, LANES:].astype(jnp.float32)
        odd = back[part + 1, :, LANES:].astype(jnp.float32)
        keys.append(jnp.where(left, even, pltpu.roll(odd, head_dim, axis=1)).astype(jnp.bfloat16))
        values.append(jnp.where(left, pltpu.roll(even, head_dim, axis=1), odd).astype(jnp.bfloat16))
    queries = [back[part, :, :LANES] for part in range(parts)]
    grad = (
        bf16_dot(jnp.concatenate(queries, axis=1), wq_ref[...], NT)
        + bf16_dot(jnp.concatenate(keys, axis=1), wk_ref[...], NT)
        + bf16_dot(jnp.concatenate(values, axis=1), wv_ref[...], NT)
    )
    values = x_ref[...].astype(jnp.float32)
    root = inverse_root(values)
    scaled = grad * gain_ref[...]
    mean = jnp.mean(scaled * values, axis=-1, keepdims=True)
    out_ref[...] = grad_mid_ref[...] + root * scaled - values * (root * root * root * mean)


def head_products_body(sources, head_dim, scalars, *refs):
    low_ref, acts_ref, w_ref, came_ref = refs[:4]
    att_ref, refs = refs[4], refs[5:]
    token_refs, refs = refs[:7], refs[7:]
    gain_ref, grad_tokens_ref, kept_out, given_out, out_kept, out_given, proj, outer, signals = refs
    parts, rows, width = acts_ref.shape
    count = parts * rows
    core = scalars[sources]
    low = low_ref[...].reshape(count, 2 * LANES)
    turned = bf16_dot(low, acts_ref[...].reshape(count, width), TN).T
    proj[...] = turned.astype(jnp.bfloat16)
    copies = cut_copies(proj, kept_out, given_out, core, signals.at[pl.ds(0, 4)])
    gain_ref[...] = jnp.sum(turned * w_ref[...].astype(jnp.float32), axis=-1, keepdims=True)
    total = None
    came = came_ref.ready()
    for slot in range(sources):
        branch = came[scalars[slot], :, LANES:]
        term = bf16_dot(branch, att_ref[slot], TN)
        total = term if total is None else total + term
    outer[...] = total.astype(jnp.bfloat16)
    copies += cut_copies(outer, out_kept, out_given, core, signals.at[pl.ds(4, 4)])
    token_grad_body(head_dim, *token_refs, grad_tokens_ref)
    for copy in copies:
        copy.wait()


def head_products(scalars, low, acts, came, w_head, att_shards, token_inputs, head_dim):
    parts, rows, width = acts.shape
    out_width = att_shards[0].shape[1]
    return kernel_call(
        lambda *refs: head_products_body(len(att_shards), head_dim, *refs),
        scalars,
        [low, acts, w_head, came, Stack(att_shards), *token_inputs],
        [
            shape_of((width, 1), jnp.float32),
            shape_of((rows, width), jnp.float32),
        ],
        [
            pltpu.VMEM((width, 2 * LANES), jnp.bfloat16),
            pltpu.VMEM((LANES, out_width), jnp.bfloat16),
            pltpu.SemaphoreType.DMA((8,)),
        ],
        6 * parts * rows * width * LANES + 4 * rows * width * width,
        "head_products",
        (),
        [shape_of((width // 2, 2 * LANES), jnp.bfloat16)] * 2
        + [shape_of((LANES // 2, out_width), jnp.bfloat16)] * 2,
    )


def spread_body(columns, count, scalars, came_ref, *outs):
    for part in range(came_ref.shape[0]):
        for index in range(count):
            piece = came_ref[part, :, index * columns : (index + 1) * columns].astype(jnp.float32)
            outs[index][:, part * columns : (part + 1) * columns] = piece


def spread_out(scalars, came, columns, count):
    parts, rows, width = came.shape
    outs = [shape_of((rows, parts * columns), jnp.float32)] * count
    return kernel_call(
        lambda *refs: spread_body(columns, count, *refs),
        scalars,
        [came],
        outs,
        [],
        0,
        "spread_out",
    )


def joined_body(parts, head_dim, scalars, *refs):
    came_refs, outs = refs[:parts], refs[parts:-2]
    joined, signals = refs[-2:]
    copies = [
        pltpu.make_async_copy(ref.ready(), joined.at[(scalars[0] + parts - at) % parts], signals.at[at])
        for at, ref in enumerate(came_refs)
    ]
    for copy in copies:
        copy.start()
    for copy in copies:
        copy.wait()
    query_ref, key_ref, value_ref, gain_ref = outs
    total = None
    for part in range(parts):
        piece = joined[part, :, : 2 * LANES].astype(jnp.float32)
        query_ref[:, part * LANES : (part + 1) * LANES] = piece[:, :LANES]
        at = slice(part * head_dim, (part + 1) * head_dim)
        key_ref[:, at] = piece[:, LANES : LANES + head_dim]
        value_ref[:, at] = piece[:, LANES + head_dim :]
        gain = joined[part, :, 2 * LANES :].astype(jnp.float32)
        total = gain if total is None else total + gain
    gain_ref[...] = total


def joined_out(scalars, came, head_dim):
    parts, (rows, width) = len(came), came[0].shape
    outs = [shape_of((rows, parts * size), jnp.float32) for size in (LANES, head_dim, head_dim)]
    outs.append(shape_of((rows, width - 2 * LANES), jnp.float32))
    return kernel_call(
        lambda *refs: joined_body(parts, head_dim, *refs),
        scalars,
        came,
        outs,
        [pltpu.VMEM((parts, rows, width), jnp.bfloat16), pltpu.SemaphoreType.DMA((parts,))],
        0,
        "joined_out",
    )


def cut_body(parts, scalars, mine_ref, got_ref, gain_ref, *refs):
    outs, (joined, signals) = refs[:parts], refs[parts:]
    each = joined.shape[1]
    width = mine_ref.shape[1]
    total = mine_ref[...].astype(jnp.float32) + got_ref[...].astype(jnp.float32)
    joined[:, :, :width] = total.astype(jnp.bfloat16).reshape(parts, each, width)
    for part in range(parts):
        joined[part, :, width:] = gain_ref[...]
    copies = [
        pltpu.make_async_copy(joined.at[(scalars[0] + at) % parts], out, signals.at[at])
        for at, out in enumerate(outs)
    ]
    for copy in copies:
        copy.start()
    for copy in copies:
        copy.wait()


def cut_blocks(scalars, mine, got, gains, parts):
    rows, width = mine.shape
    each = rows // parts
    total = width + gains.shape[1]
    outs = [shape_of((each, total), jnp.bfloat16)] * parts
    return kernel_call(
        lambda *refs: cut_body(parts, *refs),
        scalars,
        [mine, got, gains],
        [],
        [pltpu.VMEM((parts, each, total), jnp.bfloat16), pltpu.SemaphoreType.DMA((parts,))],
        0,
        "cut_blocks",
        (),
        outs,
    )


def swapped(value, axis, by):
    count = lax.axis_size(axis)
    return lax.ppermute(value, axis, [(i, i ^ by) for i in range(count)])


def after(value, *others):
    return lax.optimization_barrier((value, *others))[0]


def split_form(
    tokens,
    lengths,
    attn_gain,
    q_gain,
    k_gain,
    w_query,
    w_key,
    w_value,
    w_out,
    ffn_gain,
    w_gate,
    w_up,
    w_down,
    cotangent,
):
    _, rows, width = tokens.shape
    head_dim = q_gain.shape[0]
    hidden_width = w_gate.shape[1]
    parts = lax.axis_size("ctx")
    sums = lax.axis_size("dp")
    place = lax.axis_index("ctx").astype(jnp.int32)
    row = lax.axis_index("dp").astype(jnp.int32)
    core, line = row % 2, row // 2
    length = lengths[0]
    columns = hidden_width // parts
    each = width // (sums * parts)
    steps = parts // 2
    sources = [((place - 2 * (slot // 2)) % parts) ^ (slot % 2) for slot in range(parts)]
    freq = THETA ** (-(jnp.arange(head_dim // 2, dtype=jnp.float32) * 2.0 / head_dim))
    sign = jnp.ones_like(freq)
    freq = jnp.stack([jnp.concatenate([freq] * 4), jnp.concatenate([-sign, sign, -sign, sign])])
    base = jnp.arange(rows, dtype=jnp.float32)[:, None] * freq[0:1]
    base = jnp.stack([jnp.cos(base), jnp.sin(base)])
    attn_row, ffn_row = attn_gain[None], ffn_gain[None]
    q_row = jnp.concatenate([q_gain, q_gain])[None]
    k_row = jnp.concatenate([k_gain, k_gain])[None]
    x_own, cot_own = tokens[0], cotangent[0]

    def own_columns(weights, size, axis):
        return lax.dynamic_slice_in_dim(weights, place * size, size, axis)

    w_head = jnp.concatenate(
        [
            own_columns(w_query, LANES, 1),
            own_columns(w_key, head_dim, 1),
            own_columns(w_value, head_dim, 1),
        ],
        axis=-1,
    )
    spare = -columns % LANES
    wide = columns + spare
    gate_up = jnp.concatenate(
        [
            jnp.pad(own_columns(w_gate, columns, 1), ((0, 0), (0, spare))),
            jnp.pad(own_columns(w_up, columns, 1), ((0, 0), (0, spare))),
        ],
        axis=-1,
    )
    down = jnp.pad(own_columns(w_down, columns, 0), ((0, spare), (0, 0)))

    half = parts // 2
    kv_weights = [w_key, w_value, attn_row, k_row, freq, base]

    def key_values(low, high, held):
        return key_value_part(
            jnp.stack(sources[low:high]), x_shards[low:high], kv_weights, parts, head_dim, held
        )

    held, x_shards, early = x_own, [], None
    for step in range(steps):
        if step:
            held = from_behind(held, "ctx", 2)
        other = held
        if step == steps - 1:
            early = key_values(0, half, ())
            other = after(held, early[0], gate_up, down, w_head, x_shards[-1])
        x_shards += [held, swapped(other, "ctx", 1)]
    fresh = 2 if parts - 2 > half else parts - half
    if parts - fresh > half:
        early = key_values(half, parts - fresh, early)
    attn_low, acts = attend(
        jnp.stack(sources + [place, length]),
        x_shards[parts - fresh :],
        x_own,
        early,
        kv_weights,
        w_query,
        q_row,
        head_dim,
    )
    where = jnp.stack([place, length])

    def along(shard):
        return [shard] + [from_behind(shard, "ctx", 2 * step) for step in range(1, steps)]

    def across(shards):
        if len(shards) == 1:
            return [swapped(shards[0], "ctx", 1)]
        joined = swapped(jnp.stack(shards), "ctx", 1)
        return [Part(joined, at) for at in range(len(shards))]

    def arrays_of(shards):
        return [shard.array if isinstance(shard, Part) else shard for shard in shards]

    cot_ready = after(cot_own, *x_shards[-2:])
    cot_along = along(cot_ready)
    cot_across = across(cot_along[:1])
    attn_low = after(attn_low, *cot_along, *cot_across)
    att_along = along(attn_low)
    att_across = across(att_along[:1])
    cot_across += across([after(shard, attn_low) for shard in cot_along[1:]])
    chunk = next(c for c in (512, 384, 256, 128) if hidden_width % c == 0)
    turned_to = sources[0::2] + sources[1::2]
    slots = jnp.stack(turned_to + [core, length])
    weights = [w_out, ffn_row, gate_up, down]
    x_along, x_across = x_shards[0::2], x_shards[1::2]
    result, grad_mid, sent, ffn_gain_part = ffn_part(
        where,
        [x_own, attn_low, cot_own, w_out, ffn_row],
        [w_gate, w_up, w_down],
        (0, hidden_width // chunk),
        chunk,
        [],
        True,
        parts,
        sums,
    )
    sent = after(sent, *att_along[1:], *att_across, *arrays_of(cot_across[1:2]))
    came = lax.all_to_all(sent, "ctx", 0, 0, tiled=True)
    att_across += across([after(shard, sent) for shard in att_along[1:]])
    factors = [
        factor_part(
            jnp.stack(turned_to[:steps] + [length]),
            [after(x_along[0], sent)] + x_along[1:],
            att_along,
            cot_along,
            weights,
        )
    ]
    came = after(came, factors[0][0], *arrays_of(att_across[1:2]))
    low, head_gains = head_gradients(
        where, acts, w_head, q_row, k_row, freq, base, came, head_dim
    )
    back = lax.all_to_all(low, "ctx", 0, 0, tiled=True)
    def core_sum(kept, given):
        total = kept.astype(jnp.float32) + swapped(given, "dp", 1).astype(jnp.float32)
        return total.astype(jnp.bfloat16)

    def line_halves(half):
        size = half.shape[0] // 2
        mine = lax.dynamic_slice_in_dim(half, line * size, size, 0)
        return mine, lax.dynamic_slice_in_dim(half, (1 - line) * size, size, 0)

    def line_sum(half):
        mine, other = line_halves(half)
        return mine.astype(jnp.float32) + swapped(other, "dp", 2).astype(jnp.float32)

    kept, given = last_products(
        jnp.stack(turned_to[steps:] + [length, core]),
        [after(x_across[0], low)] + x_across[1:],
        att_across,
        cot_across,
        weights,
        factors,
        columns,
    )
    wide_half = core_sum(kept, after(given, back))
    wide_mine, wide_other = line_halves(wide_half)
    wide_got = swapped(wide_other, "dp", 2)
    attn_part, grad_tokens, head_kept, head_given, out_kept, out_given = head_products(
        slots,
        after(low, wide_other),
        acts,
        came,
        w_head,
        att_along + att_across,
        [back, w_query, w_key, w_value, x_own, grad_mid, attn_row],
        head_dim,
    )
    wide_sum = after(wide_mine, head_kept).astype(jnp.float32) + wide_got.astype(jnp.float32)
    wide_sum = wide_sum.astype(jnp.bfloat16).reshape(parts, each, -1)
    wide_came = lax.all_to_all(wide_sum, "ctx", 0, 0, tiled=True)
    head_half = core_sum(head_kept, after(head_given, wide_sum))
    out_half = core_sum(out_kept, after(out_given, wide_sum))
    gains = jnp.concatenate(
        [
            attn_part[:, 0] / attn_gain,
            ffn_gain_part[0],
            head_gains[0, :head_dim] + head_gains[0, head_dim:],
            head_gains[1, :head_dim],
        ]
    )
    gain_count = gains.shape[0]
    gains = after(gains, wide_sum)
    gains = gains + swapped(gains, "dp", 1)
    head_mine, head_other = line_halves(head_half)

    def high_low(values, columns_at):
        high = lax.reduce_precision(values, 8, 7)
        both = jnp.concatenate([high, values - high]).astype(jnp.bfloat16)
        room = -(-both.shape[0] // (16 * columns_at)) * 16
        return jnp.pad(both, (0, room * columns_at - both.shape[0])).reshape(room, columns_at)

    packed = jnp.concatenate([head_other, high_low(gains, head_other.shape[1])])
    got = swapped(packed, "dp", 2)
    head_got, gains_got = got[: head_other.shape[0]], got[head_other.shape[0] :].reshape(-1)
    gains = gains + gains_got[:gain_count].astype(jnp.float32)
    gains = gains + gains_got[gain_count : 2 * gain_count].astype(jnp.float32)
    out_sum = line_sum(out_half)
    pieces = high_low(gains, each * LANES // 32).reshape(-1)
    room = -(-pieces.shape[0] // (each * LANES)) * LANES
    pieces = jnp.pad(pieces, (0, each * room - pieces.shape[0])).reshape(each, room)
    leaving = cut_blocks(place[None], head_mine, head_got, pieces, parts)
    last = [leaving[0]] + [from_behind(leaving[at], "ctx", at) for at in range(1, parts)]
    query_out, key_out, value_out, totals = joined_out(place[None], last, head_dim)
    gate_sum, up_sum, down_out = spread_out(place[None], wide_came, columns, 3)
    totals = totals.reshape(-1)
    totals = totals[:gain_count] + totals[gain_count : 2 * gain_count]
    return (
        result[None],
        grad_tokens[None],
        totals[:width],
        totals[2 * width : 2 * width + head_dim],
        totals[2 * width + head_dim :],
        query_out,
        key_out,
        value_out,
        out_sum.T,
        totals[width : 2 * width],
        gate_sum,
        up_sum,
        down_out.T,
    )


def per_device(*arguments):
    tokens, q_gain, w_query, w_key = (arguments[i] for i in (0, 3, 5, 6))
    parts = lax.axis_size("ctx")
    sums = lax.axis_size("dp")
    head_dim = q_gain.shape[0]
    fits = (
        tokens.shape[0] == 1
        and sums == 4
        and parts % 2 == 0
        and 2 * head_dim == LANES
        and w_query.shape[1] == parts * LANES
        and w_key.shape[1] == parts * head_dim
        and tokens.shape[2] == sums * parts * 32
        and tokens.shape[1] == LANES
        and parts <= 8
    )
    return (split_form if fits else ring_form)(*arguments)


def solution(mesh):
    placed = (
        P("dp", "ctx", None),
        P("dp"),
        P(),
        P(),
        P(),
        P(),
        P(),
        P(),
        P(),
        P(),
        P(),
        P(),
        P(),
        P("dp", "ctx", None),
    )
    return jax.shard_map(
        per_device,
        mesh=mesh,
        in_specs=placed,
        out_specs=(
            P("dp", "ctx", None),
            P("dp", "ctx", None),
            P(),
            P(),
            P(),
            P(("dp", "ctx"), None),
            P(("dp", "ctx"), None),
            P(("dp", "ctx"), None),
            P(None, ("dp", "ctx")),
            P(),
            P(("dp", "ctx"), None),
            P(("dp", "ctx"), None),
            P(None, ("dp", "ctx")),
        ),
        check_vma=False,
    )
```

profile of v0, /device:TPU:18, one launch (start us, length us, event | category | flops | bytes accessed | tf_op | source)
XLA Modules:
  0.0 232.2 jit_solution(4186731562542854764)
XLA Ops:
  3.8 3.2 %constant_dynamic-slice_fusion.9 = (bf16[1024,576]{1,0:T(8,128)(2,1)S(1)}, bf16[1024,576]{1,0:T(8,128)(2,1)S(1)}) fusion(bf16[1024,4608]{1,0:T(8,128)(2,1)} %refs_7_.1, s32[]{:T(128)S(6)} %select_n.65, bf16[1024,4608]{1,0:T(8,128)(2,1)} %refs_6_.1), kind=kLoop, calls=%fused_computation.44 | loop fusion | bytes 4718596 | tf_op jit(solution)/shard_map/dynamic_slice | solution.py:1245
  7.1 1.7 fusion.2.refs_14_
  13.2 1.8 collective-permute-start.4
  15.6 3.3 %collective-permute-done.1.refs_0_.refs_2_ = bf16[128,1024]{1,0:T(8,128)(2,1)S(1)} collective-permute-done((bf16[128,1024]{1,0:T(8,128)(2,1)}, bf16[128,1024]{1,0:T(8,128)(2,1)S(1)}, u32[]{:S(2)}, u32[]{:S(2)}) %collective-permute-start.1) | collective-permute-done | bytes 262176 | tf_op jit(solution)/shard_map/ppermute | solution.py:24
  24.2 6.5 %key_value_part.2 = (bf16[8,128,1024]{2,1,0:T(8,128)(2,1)}, bf16[8,128,1024]{2,1,0:T(8,128)(2,1)}) custom-call(s32[4]{0:T(128)} %pad_add_fusion.1.scalars_ref, bf16[128,1024]{1,0:T(8,128)(2,1)} %bitcast.44, bf16[128,1024]{1,0:T(8,128)(2,1)} %copy-done.29, bf16[128,1024]{1,0:T(8,128)(2,1)} %collective-permute-done.refs_2_.refs_1_, ...), custom_call_target="tpu_custom_call" | custom-call | flops 1073741824 | bytes 7476736 | tf_op jit(solution)/shard_map/key_value_part/pallas_call | solution.py:467
  33.2 4.6 %collective-permute-done.6.refs_1_.refs_3_ = bf16[128,1024]{1,0:T(8,128)(2,1)S(1)} collective-permute-done((bf16[128,1024]{1,0:T(8,128)(2,1)S(1)}, bf16[128,1024]{1,0:T(8,128)(2,1)S(1)}, u32[]{:S(2)}, u32[]{:S(2)}) %collective-permute-start.6) | collective-permute-done | bytes 262176 | tf_op jit(solution)/shard_map/ppermute | solution.py:1198
  38.1 1.9 collective-permute-start.9
  40.0 4.0 %collective-permute-start.8 = (bf16[128,1024]{1,0:T(8,128)(2,1)S(1)}, bf16[128,1024]{1,0:T(8,128)(2,1)S(1)}, u32[]{:S(2)}, u32[]{:S(2)}) collective-permute-start(bf16[128,1024]{1,0:T(8,128)(2,1)S(1)} %bitcast.56), channel_id=1, source_target_pairs={{0,4},{1,5},{2,6},{3,7},{4,0},{5,1},{6,2},{7,3},{8,12},{9,13},{10,... | collective-permute-start | bytes 786440 | tf_op jit(solution)/shard_map/ppermute | solution.py:24
  44.6 4.7 %key_value_part.3 = (bf16[8,128,1024]{2,1,0:T(8,128)(2,1)}, bf16[8,128,1024]{2,1,0:T(8,128)(2,1)}) custom-call(s32[2]{0:T(128)} %pad_add_fusion.2.scalars_ref, bf16[128,1024]{1,0:T(8,128)(2,1)} %copy-done.10, bf16[128,1024]{1,0:T(8,128)(2,1)} %copy-done.11, bf16[1024,512]{1,0:T(8,128)(2,1)} %refs_14_.1, ...), custom_call_target="tpu_custom_call", output_to_operand_aliasing={{0}: (9, {}), {1}: (10, {})} | custom-call | flops 536870912 | bytes 6952448 | tf_op jit(solution)/shard_map/key_value_part/pallas_call | solution.py:467
  49.3 13.7 %attend.1 = (bf16[128,1024]{1,0:T(8,128)(2,1)}, bf16[8,128,1024]{2,1,0:T(8,128)(2,1)}) custom-call(s32[10]{0:T(128)} %stack.120.scalars_ref, bf16[128,1024]{1,0:T(8,128)(2,1)} %copy-done.9, bf16[128,1024]{1,0:T(8,128)(2,1)} %copy-done.8, bf16[1024,512]{1,0:T(8,128)(2,1)} %refs_14_.1, bf16[1024,512]{1,0:T(8,128)(2,1)} %refs_15_.1, ...), custom_call_target="tpu_custom_call", output_to_operand_aliasing={{1}: (18, {})} | custom-call | flops 1342177280 | bytes 20060160 | tf_op jit(solution)/shard_map/attend/pallas_call | solution.py:467
  66.5 2.0 collective-permute-start.13
  68.6 1.8 collective-permute-start.12
  70.4 22.3 %ffn_part.1 = (bf16[128,1024]{1,0:T(8,128)(2,1)}, f32[128,1024]{1,0:T(8,128)}, bf16[8,128,256]{2,1,0:T(8,128)(2,1)}, f32[1,1024]{1,0:T(1,128)}) custom-call(s32[2]{0:T(128)} %pad_add_fusion.refs_0_.scalars_ref, bf16[128,1024]{1,0:T(8,128)(2,1)} %bitcast.46, bf16[128,1024]{1,0:T(8,128)(2,1)} %get-tuple-element.79.refs_2_.refs_4_, bf16[128,1024]{1,0:T(8,128)(2,1)} %bitcast.52, ...), custom_call_target="tpu_custom_call" | custom-call | flops 7247757312 | bytes 28311552 | tf_op jit(solution)/shard_map/ffn_part/pallas_call | solution.py:779
  93.8 7.1 %all-to-all-start = ((bf16[8,128,256]{2,1,0:T(8,128)(2,1)}), bf16[8,128,256]{2,1,0:T(8,128)(2,1)S(1)}, u32[]{:S(2)}, u32[]{:S(2)}) async-start(bf16[8,128,256]{2,1,0:T(8,128)(2,1)} %get-tuple-element.86), calls=%async_computation | async-start | bytes 1048576 | tf_op jit(solution)/shard_map/all_to_all | solution.py:1334
  102.3 10.0 %factor_part.1 = (bf16[512,1024]{1,0:T(8,128)(2,1)}, bf16[512,1024]{1,0:T(8,128)(2,1)}, bf16[512,640]{1,0:T(8,128)(2,1)}, bf16[512,640]{1,0:T(8,128)(2,1)}, bf16[512,640]{1,0:T(8,128)(2,1)}) custom-call(s32[5]{0:T(128)} %stack.132.scalars_ref, bf16[128,1024]{1,0:T(8,128)(2,1)} %bitcast.47, bf16[128,1024]{1,0:T(8,128)(2,1)} %collective-permute-done.refs_2_.refs_1_, ...), custom_call_target="tpu_custom_call" | custom-call | flops 3087007744 | bytes 13242368 | tf_op jit(solution)/shard_map/factor_part/pallas_call | solution.py:467
  112.4 6.6 %collective-permute-done.16.refs_5_.refs_6_.refs_7_.refs_9_.refs_10_.refs_11_ = bf16[3,128,1024]{2,1,0:T(8,128)(2,1)S(1)} collective-permute-done((bf16[3,128,1024]{2,1,0:T(8,128)(2,1)S(1)}, bf16[3,128,1024]{2,1,0:T(8,128)(2,1)S(1)}, u32[]{:S(2)}, u32[]{:S(2)}) %collective-permute-start.16) | collective-permute-done | bytes 786464 | tf_op jit(solution)/shard_map/ppermute | solution.py:1198
  119.8 14.8 %head_gradients.1 = (bf16[8,128,256]{2,1,0:T(8,128)(2,1)}, f32[8,128]{1,0:T(8,128)}) custom-call(s32[2]{0:T(128)} %pad_add_fusion.refs_0_.scalars_ref, bf16[1024,256]{1,0:T(8,128)(2,1)} %pad_maximum_fusion.2.refs_0_.refs_2_, f32[1,128]{1,0:T(1,128)} %maximum_bitcast_fusion.1.refs_10_.refs_1_, f32[1,128]{1,0:T(1,128)} %maximum_bitcast_fusion.refs_7_.refs_5_.refs_2_, ...), custom_call_target="tpu_custom_call" | custom-call | flops 1476395008 | bytes 3807232 | tf_op jit(solution)/shard_map/head_gradients/pallas_call | solution.py:467
  134.6 6.0 %all-to-all-start.1 = ((bf16[8,128,256]{2,1,0:T(8,128)(2,1)}), bf16[8,128,256]{2,1,0:T(8,128)(2,1)S(1)}, u32[]{:S(2)}, u32[]{:S(2)}) async-start(bf16[8,128,256]{2,1,0:T(8,128)(2,1)} %get-tuple-element.102.refs_0_), calls=%async_computation.1 | async-start | bytes 1048576 | tf_op jit(solution)/shard_map/all_to_all | solution.py:1349
  141.2 16.2 %last_products.1 = (bf16[512,1792]{1,0:T(8,128)(2,1)}, bf16[512,1792]{1,0:T(8,128)(2,1)}) custom-call(s32[6]{0:T(128)} %stack.137.scalars_ref, bf16[128,1024]{1,0:T(8,128)(2,1)} %copy-done.29, bf16[128,1024]{1,0:T(8,128)(2,1)} %collective-permute-done.4.refs_3_.refs_1_, bf16[128,1024]{1,0:T(8,128)(2,1)} %copy-done.11, bf16[128,1024]{1,0:T(8,128)(2,1)} %copy-done.8, ...), custom_call_target="tpu_custom_call" | custom-call | flops 6710886400 | bytes 16912384 | tf_op jit(solution)/shard_map/last_products/pallas_call | solution.py:467
  157.6 4.0 %collective-permute-done.17 = bf16[512,1792]{1,0:T(8,128)(2,1)S(1)} collective-permute-done((bf16[512,1792]{1,0:T(8,128)(2,1)}, bf16[512,1792]{1,0:T(8,128)(2,1)S(1)}, u32[]{:S(2)}, u32[]{:S(2)}) %collective-permute-start.17) | collective-permute-done | bytes 1835040 | tf_op jit(solution)/shard_map/ppermute | solution.py:1198
  161.5 1.9 add_convert_fusion
  166.6 7.8 %head_products.1 = (f32[1024,1]{1,0:T(8,128)}, f32[128,1024]{1,0:T(8,128)}, bf16[512,256]{1,0:T(8,128)(2,1)}, bf16[512,256]{1,0:T(8,128)(2,1)}, bf16[64,1024]{1,0:T(8,128)(2,1)}, /*index=5*/bf16[64,1024]{1,0:T(8,128)(2,1)}) custom-call(s32[10]{0:T(128)} %stack.127.scalars_ref, bf16[8,128,256]{2,1,0:T(8,128)(2,1)} %get-tuple-element.102.refs_0_, ...), custom_call_target="tpu_custom_call" | custom-call | flops 1342177280 | bytes 12591104 | tf_op jit(solution)/shard_map/head_products/pallas_call | solution.py:467
  175.8 10.2 %collective-permute-done.18 = bf16[256,1792]{1,0:T(8,128)(2,1)S(1)} collective-permute-done((bf16[256,1792]{1,0:T(8,128)(2,1)S(1)}, bf16[256,1792]{1,0:T(8,128)(2,1)S(1)}, u32[]{:S(2)}, u32[]{:S(2)}) %collective-permute-start.18) | collective-permute-done | bytes 917536 | tf_op jit(solution)/shard_map/ppermute | solution.py:1198
  187.2 6.2 %all-to-all-start.2 = ((bf16[8,32,1792]{2,1,0:T(8,128)(2,1)}), bf16[8,32,1792]{2,1,0:T(8,128)(2,1)S(1)}, u32[]{:S(2)}, u32[]{:S(2)}) async-start(bf16[8,32,1792]{2,1,0:T(8,128)(2,1)} %bitcast.25), calls=%async_computation.2 | async-start | bytes 1835008 | tf_op jit(solution)/shard_map/all_to_all | solution.py:1387
  198.1 4.5 %collective-permute-done.21 = bf16[288,256]{1,0:T(8,128)(2,1)S(1)} collective-permute-done((bf16[288,256]{1,0:T(8,128)(2,1)S(1)}, bf16[288,256]{1,0:T(8,128)(2,1)S(1)}, u32[]{:S(2)}, u32[]{:S(2)}) %collective-permute-start.21) | collective-permute-done | bytes 147488 | tf_op jit(solution)/shard_map/ppermute | solution.py:1198
  203.9 1.8 cut_blocks.1
  207.3 2.0 collective-permute-start.24
  209.2 2.4 %collective-permute-start.25 = (bf16[32,512]{1,0:T(8,128)(2,1)}, bf16[32,512]{1,0:T(8,128)(2,1)S(1)}, u32[]{:S(2)}, u32[]{:S(2)}) collective-permute-start(bf16[32,512]{1,0:T(8,128)(2,1)} %get-tuple-element.117), channel_id=1, source_target_pairs={{0,4},{1,5},{2,6},{3,7},{4,0},{5,1},{6,2},{7,3},{8,12},{9,13},{10,... | collective-permute-start | bytes 98312 | tf_op jit(solution)/shard_map/ppermute | solution.py:24
  213.1 4.3 %collective-permute-start.27 = (bf16[32,512]{1,0:T(8,128)(2,1)}, bf16[32,512]{1,0:T(8,128)(2,1)S(1)}, u32[]{:S(2)}, u32[]{:S(2)}) collective-permute-start(bf16[32,512]{1,0:T(8,128)(2,1)} %get-tuple-element.119), channel_id=1, source_target_pairs={{0,6},{1,7},{2,0},{3,1},{4,2},{5,3},{6,4},{7,5},{8,14},{9,15},{10,... | collective-permute-start | bytes 98312 | tf_op jit(solution)/shard_map/ppermute | solution.py:24
  220.0 3.8 %collective-permute-done.28.refs_7_ = bf16[32,512]{1,0:T(8,128)(2,1)S(1)} collective-permute-done((bf16[32,512]{1,0:T(8,128)(2,1)}, bf16[32,512]{1,0:T(8,128)(2,1)S(1)}, u32[]{:S(2)}, u32[]{:S(2)}) %collective-permute-start.28) | collective-permute-done | bytes 32800 | tf_op jit(solution)/shard_map/ppermute | solution.py:24
  224.4 2.1 joined_out.1
  229.4 2.6 %spread_out.1 = (f32[32,4608]{1,0:T(8,128)}, f32[32,4608]{1,0:T(8,128)}, f32[32,4608]{1,0:T(8,128)}) custom-call(s32[1]{0:T(128)} %bitcast.scalars_ref, bf16[8,32,1792]{2,1,0:T(8,128)(2,1)} %copy-done.1), custom_call_target="tpu_custom_call" | custom-call | bytes 2686976 | tf_op jit(solution)/shard_map/spread_out/pallas_call | solution.py:467
  (167 shorter events, 44.2 us)
Async XLA Ops:
  0.6 22.8 %collective-permute-start.3 = (bf16[128,1024]{1,0:T(8,128)(2,1)}, bf16[128,1024]{1,0:T(8,128)(2,1)S(1)}, u32[]{:S(2)}, u32[]{:S(2)}) collective-permute-start(bf16[128,1024]{1,0:T(8,128)(2,1)} %bitcast.42), channel_id=1, source_target_pairs={{0,1},{1,0},{2,3},{3,2},{4,5},{5,4},{6,7},{7,6},{8,9},{9,8},{10,11... | collective-permute-start | bytes 786440 | tf_op jit(solution)/shard_map/ppermute | solution.py:1198
  1.2 9.9 %collective-permute-start = (bf16[128,1024]{1,0:T(8,128)(2,1)}, bf16[128,1024]{1,0:T(8,128)(2,1)}, u32[]{:S(2)}, u32[]{:S(2)}) collective-permute-start(bf16[128,1024]{1,0:T(8,128)(2,1)} %bitcast.43), channel_id=1, source_target_pairs={{0,2},{1,3},{2,4},{3,5},{4,6},{5,7},{6,0},{7,1},{8,10},{9,11},{10,... | collective-permute-start | bytes 786440 | tf_op jit(solution)/shard_map/ppermute | solution.py:24
  11.2 7.7 %collective-permute-start.1 = (bf16[128,1024]{1,0:T(8,128)(2,1)}, bf16[128,1024]{1,0:T(8,128)(2,1)S(1)}, u32[]{:S(2)}, u32[]{:S(2)}) collective-permute-start(bf16[128,1024]{1,0:T(8,128)(2,1)} %collective-permute-done.refs_2_.refs_1_), channel_id=1, source_target_pairs={{0,2},{1,3},{2,4},{3,5},{4,6},{5,7},{6,0},{7,1},{8,10},{9,11},{10,... | collective-permute-start | bytes 786440 | tf_op jit(solution)/shard_map/ppermute | solution.py:24
  13.2 10.3 %collective-permute-start.4 = (bf16[128,1024]{1,0:T(8,128)(2,1)}, bf16[128,1024]{1,0:T(8,128)(2,1)}, u32[]{:S(2)}, u32[]{:S(2)}) collective-permute-start(bf16[128,1024]{1,0:T(8,128)(2,1)} %collective-permute-done.refs_2_.refs_1_), channel_id=1, source_target_pairs={{0,1},{1,0},{2,3},{3,2},{4,5},{5,4},{6,7},{7,6},{8,9},{9,8},{10,11... | collective-permute-start | bytes 786440 | tf_op jit(solution)/shard_map/ppermute | solution.py:1198
  18.9 11.7 %collective-permute-start.5 = (bf16[128,1024]{1,0:T(8,128)(2,1)S(1)}, bf16[128,1024]{1,0:T(8,128)(2,1)S(1)}, u32[]{:S(2)}, u32[]{:S(2)}) collective-permute-start(bf16[128,1024]{1,0:T(8,128)(2,1)S(1)} %collective-permute-done.1.refs_0_.refs_2_), channel_id=1, source_target_pairs={{0,1},{1,0},{2,3},{3,2},{4,5},{5,4},{6,7},{7,6},{8,9},{9,8},{10,11... | collective-permute-start | bytes 786440 | tf_op jit(solution)/shard_map/ppermute | solution.py:1198
  20.4 10.3 %collective-permute-start.2 = (bf16[128,1024]{1,0:T(8,128)(2,1)S(1)}, bf16[128,1024]{1,0:T(8,128)(2,1)S(1)}, u32[]{:S(2)}, u32[]{:S(2)}) collective-permute-start(bf16[128,1024]{1,0:T(8,128)(2,1)S(1)} %collective-permute-done.1.refs_0_.refs_2_), channel_id=1, source_target_pairs={{0,2},{1,3},{2,4},{3,5},{4,6},{5,7},{6,0},{7,1},{8,10},{9,11},{10,... | collective-permute-start | bytes 786440 | tf_op jit(solution)/shard_map/ppermute | solution.py:24
  30.7 7.1 %collective-permute-start.6 = (bf16[128,1024]{1,0:T(8,128)(2,1)S(1)}, bf16[128,1024]{1,0:T(8,128)(2,1)S(1)}, u32[]{:S(2)}, u32[]{:S(2)}) collective-permute-start(bf16[128,1024]{1,0:T(8,128)(2,1)S(1)} %collective-permute-done.2.refs_0_.refs_3_), channel_id=1, source_target_pairs={{0,1},{1,0},{2,3},{3,2},{4,5},{5,4},{6,7},{7,6},{8,9},{9,8},{10,11... | collective-permute-start | bytes 786440 | tf_op jit(solution)/shard_map/ppermute | solution.py:1198
  37.8 25.3 %collective-permute-start.10 = (bf16[128,1024]{1,0:T(8,128)(2,1)S(1)}, bf16[128,1024]{1,0:T(8,128)(2,1)S(1)}, u32[]{:S(2)}, u32[]{:S(2)}) collective-permute-start(bf16[128,1024]{1,0:T(8,128)(2,1)S(1)} %bitcast.54), channel_id=1, source_target_pairs={{0,1},{1,0},{2,3},{3,2},{4,5},{5,4},{6,7},{7,6},{8,9},{9,8},{10,11... | collective-permute-start | bytes 786440 | tf_op jit(solution)/shard_map/ppermute | solution.py:1198
  38.1 25.0 %collective-permute-start.9 = (bf16[128,1024]{1,0:T(8,128)(2,1)S(1)}, bf16[128,1024]{1,0:T(8,128)(2,1)S(1)}, u32[]{:S(2)}, u32[]{:S(2)}) collective-permute-start(bf16[128,1024]{1,0:T(8,128)(2,1)S(1)} %bitcast.55), channel_id=1, source_target_pairs={{0,6},{1,7},{2,0},{3,1},{4,2},{5,3},{6,4},{7,5},{8,14},{9,15},{10,... | collective-permute-start | bytes 786440 | tf_op jit(solution)/shard_map/ppermute | solution.py:24
  40.0 23.1 %collective-permute-start.8 = (bf16[128,1024]{1,0:T(8,128)(2,1)S(1)}, bf16[128,1024]{1,0:T(8,128)(2,1)S(1)}, u32[]{:S(2)}, u32[]{:S(2)}) collective-permute-start(bf16[128,1024]{1,0:T(8,128)(2,1)S(1)} %bitcast.56), channel_id=1, source_target_pairs={{0,4},{1,5},{2,6},{3,7},{4,0},{5,1},{6,2},{7,3},{8,12},{9,13},{10,... | collective-permute-start | bytes 786440 | tf_op jit(solution)/shard_map/ppermute | solution.py:24
  44.0 19.1 %collective-permute-start.7 = (bf16[128,1024]{1,0:T(8,128)(2,1)S(1)}, bf16[128,1024]{1,0:T(8,128)(2,1)S(1)}, u32[]{:S(2)}, u32[]{:S(2)}) collective-permute-start(bf16[128,1024]{1,0:T(8,128)(2,1)S(1)} %bitcast.57), channel_id=1, source_target_pairs={{0,2},{1,3},{2,4},{3,5},{4,6},{5,7},{6,0},{7,1},{8,10},{9,11},{10,... | collective-permute-start | bytes 786440 | tf_op jit(solution)/shard_map/ppermute | solution.py:24
  63.9 29.0 %collective-permute-start.15 = (bf16[3,128,1024]{2,1,0:T(8,128)(2,1)S(1)}, bf16[3,128,1024]{2,1,0:T(8,128)(2,1)S(1)}, u32[]{:S(2)}, u32[]{:S(2)}) collective-permute-start(bf16[3,128,1024]{2,1,0:T(8,128)(2,1)S(1)} %pad_maximum_fusion), channel_id=1, source_target_pairs={{0,1},{1,0},{2,3},{3,2},{4,5},{5,4},{6,7},{7,6},{8,9},{9,8},{10,11... | collective-permute-start | bytes 2359304 | tf_op jit(solution)/shard_map/ppermute | solution.py:1198
  66.0 26.7 %collective-permute-start.14 = (bf16[128,1024]{1,0:T(8,128)(2,1)}, bf16[128,1024]{1,0:T(8,128)(2,1)S(1)}, u32[]{:S(2)}, u32[]{:S(2)}) collective-permute-start(bf16[128,1024]{1,0:T(8,128)(2,1)} %get-tuple-element.79.refs_2_.refs_4_), channel_id=1, source_target_pairs={{0,1},{1,0},{2,3},{3,2},{4,5},{5,4},{6,7},{7,6},{8,9},{9,8},{10,11... | collective-permute-start | bytes 786440 | tf_op jit(solution)/shard_map/ppermute | solution.py:1198
  66.5 26.2 %collective-permute-start.13 = (bf16[128,1024]{1,0:T(8,128)(2,1)}, bf16[128,1024]{1,0:T(8,128)(2,1)S(1)}, u32[]{:S(2)}, u32[]{:S(2)}) collective-permute-start(bf16[128,1024]{1,0:T(8,128)(2,1)} %get-tuple-element.79.refs_2_.refs_4_), channel_id=1, source_target_pairs={{0,6},{1,7},{2,0},{3,1},{4,2},{5,3},{6,4},{7,5},{8,14},{9,15},{10,... | collective-permute-start | bytes 786440 | tf_op jit(solution)/shard_map/ppermute | solution.py:24
  68.6 24.2 %collective-permute-start.12 = (bf16[128,1024]{1,0:T(8,128)(2,1)}, bf16[128,1024]{1,0:T(8,128)(2,1)S(1)}, u32[]{:S(2)}, u32[]{:S(2)}) collective-permute-start(bf16[128,1024]{1,0:T(8,128)(2,1)} %get-tuple-element.79.refs_2_.refs_4_), channel_id=1, source_target_pairs={{0,4},{1,5},{2,6},{3,7},{4,0},{5,1},{6,2},{7,3},{8,12},{9,13},{10,... | collective-permute-start | bytes 786440 | tf_op jit(solution)/shard_map/ppermute | solution.py:24
  70.4 22.4 %collective-permute-start.11 = (bf16[128,1024]{1,0:T(8,128)(2,1)}, bf16[128,1024]{1,0:T(8,128)(2,1)S(1)}, u32[]{:S(2)}, u32[]{:S(2)}) collective-permute-start(bf16[128,1024]{1,0:T(8,128)(2,1)} %get-tuple-element.79.refs_2_.refs_4_), channel_id=1, source_target_pairs={{0,2},{1,3},{2,4},{3,5},{4,6},{5,7},{6,0},{7,1},{8,10},{9,11},{10,... | collective-permute-start | bytes 786440 | tf_op jit(solution)/shard_map/ppermute | solution.py:24
  93.8 25.1 %all-to-all-start = ((bf16[8,128,256]{2,1,0:T(8,128)(2,1)}), bf16[8,128,256]{2,1,0:T(8,128)(2,1)S(1)}, u32[]{:S(2)}, u32[]{:S(2)}) async-start(bf16[8,128,256]{2,1,0:T(8,128)(2,1)} %get-tuple-element.86), calls=%async_computation | async-start | bytes 1048576 | tf_op jit(solution)/shard_map/all_to_all | solution.py:1334
  101.1 17.8 %collective-permute-start.16 = (bf16[3,128,1024]{2,1,0:T(8,128)(2,1)S(1)}, bf16[3,128,1024]{2,1,0:T(8,128)(2,1)S(1)}, u32[]{:S(2)}, u32[]{:S(2)}) collective-permute-start(bf16[3,128,1024]{2,1,0:T(8,128)(2,1)S(1)} %pad_maximum_fusion.1), channel_id=1, source_target_pairs={{0,1},{1,0},{2,3},{3,2},{4,5},{5,4},{6,7},{7,6},{8,9},{9,8},{10,11... | collective-permute-start | bytes 2359304 | tf_op jit(solution)/shard_map/ppermute | solution.py:1198
  134.6 22.8 %all-to-all-start.1 = ((bf16[8,128,256]{2,1,0:T(8,128)(2,1)}), bf16[8,128,256]{2,1,0:T(8,128)(2,1)S(1)}, u32[]{:S(2)}, u32[]{:S(2)}) async-start(bf16[8,128,256]{2,1,0:T(8,128)(2,1)} %get-tuple-element.102.refs_0_), calls=%async_computation.1 | async-start | bytes 1048576 | tf_op jit(solution)/shard_map/all_to_all | solution.py:1349
  163.6 22.5 %collective-permute-start.18 = (bf16[256,1792]{1,0:T(8,128)(2,1)S(1)}, bf16[256,1792]{1,0:T(8,128)(2,1)S(1)}, u32[]{:S(2)}, u32[]{:S(2)}) collective-permute-start(bf16[256,1792]{1,0:T(8,128)(2,1)S(1)} %get-tuple-element.134), channel_id=1, source_target_pairs={{0,16},{8,24},{16,0},{24,8},{1,17},{9,25},{17,1},{25,9},{2,18},{10... | collective-permute-start | bytes 2752520 | tf_op jit(solution)/shard_map/ppermute | solution.py:1198
  187.2 6.7 %collective-permute-start.20 = (f32[2176]{0:T(1024)S(1)}, f32[2176]{0:T(1024)S(1)}, u32[]{:S(2)}, u32[]{:S(2)}) collective-permute-start(f32[2176]{0:T(1024)S(1)} %concatenate.34), channel_id=1, source_target_pairs={{0,8},{8,0},{16,24},{24,16},{1,9},{9,1},{17,25},{25,17},{2,10},{10... | collective-permute-start | bytes 26120 | tf_op jit(solution)/shard_map/ppermute | solution.py:1198
  187.2 41.3 %all-to-all-start.2 = ((bf16[8,32,1792]{2,1,0:T(8,128)(2,1)}), bf16[8,32,1792]{2,1,0:T(8,128)(2,1)S(1)}, u32[]{:S(2)}, u32[]{:S(2)}) async-start(bf16[8,32,1792]{2,1,0:T(8,128)(2,1)} %bitcast.25), calls=%async_computation.2 | async-start | bytes 1835008 | tf_op jit(solution)/shard_map/all_to_all | solution.py:1387
  193.4 4.1 %collective-permute-start.29 = (bf16[64,1024]{1,0:T(8,128)(2,1)}, bf16[64,1024]{1,0:T(8,128)(2,1)S(1)}, u32[]{:S(2)}, u32[]{:S(2)}) collective-permute-start(bf16[64,1024]{1,0:T(8,128)(2,1)} %get-tuple-element.127), channel_id=1, source_target_pairs={{0,8},{8,0},{16,24},{24,16},{1,9},{9,1},{17,25},{25,17},{2,10},{10... | collective-permute-start | bytes 393224 | tf_op jit(solution)/shard_map/ppermute | solution.py:1198
  195.8 6.7 %collective-permute-start.21 = (bf16[288,256]{1,0:T(8,128)(2,1)S(1)}, bf16[288,256]{1,0:T(8,128)(2,1)S(1)}, u32[]{:S(2)}, u32[]{:S(2)}) collective-permute-start(bf16[288,256]{1,0:T(8,128)(2,1)S(1)} %pad_maximum_fusion.3), channel_id=1, source_target_pairs={{0,16},{8,24},{16,0},{24,8},{1,17},{9,25},{17,1},{25,9},{2,18},{10... | collective-permute-start | bytes 442376 | tf_op jit(solution)/shard_map/ppermute | solution.py:1198
  197.5 14.1 %collective-permute-start.30 = (bf16[32,1024]{1,0:T(8,128)(2,1)S(1)}, bf16[32,1024]{1,0:T(8,128)(2,1)S(1)}, u32[]{:S(2)}, u32[]{:S(2)}) collective-permute-start(bf16[32,1024]{1,0:T(8,128)(2,1)S(1)} %constant_dynamic-slice_fusion), channel_id=1, source_target_pairs={{0,16},{8,24},{16,0},{24,8},{1,17},{9,25},{17,1},{25,9},{2,18},{10... | collective-permute-start | bytes 196616 | tf_op jit(solution)/shard_map/ppermute | solution.py:1198
  205.7 7.4 %collective-permute-start.22 = (bf16[32,512]{1,0:T(8,128)(2,1)}, bf16[32,512]{1,0:T(8,128)(2,1)S(1)}, u32[]{:S(2)}, u32[]{:S(2)}) collective-permute-start(bf16[32,512]{1,0:T(8,128)(2,1)} %get-tuple-element.114), channel_id=1, source_target_pairs={{0,1},{1,2},{2,3},{3,4},{4,5},{5,6},{6,7},{7,0},{8,9},{9,10},{10,1... | collective-permute-start | bytes 98312 | tf_op jit(solution)/shard_map/ppermute | solution.py:24
  207.2 11.6 %collective-permute-start.23 = (bf16[32,512]{1,0:T(8,128)(2,1)}, bf16[32,512]{1,0:T(8,128)(2,1)S(1)}, u32[]{:S(2)}, u32[]{:S(2)}) collective-permute-start(bf16[32,512]{1,0:T(8,128)(2,1)} %get-tuple-element.115), channel_id=1, source_target_pairs={{0,2},{1,3},{2,4},{3,5},{4,6},{5,7},{6,0},{7,1},{8,10},{9,11},{10,... | collective-permute-start | bytes 98312 | tf_op jit(solution)/shard_map/ppermute | solution.py:24
  207.3 12.6 %collective-permute-start.24 = (bf16[32,512]{1,0:T(8,128)(2,1)}, bf16[32,512]{1,0:T(8,128)(2,1)S(1)}, u32[]{:S(2)}, u32[]{:S(2)}) collective-permute-start(bf16[32,512]{1,0:T(8,128)(2,1)} %get-tuple-element.116), channel_id=1, source_target_pairs={{0,3},{1,4},{2,5},{3,6},{4,7},{5,0},{6,1},{7,2},{8,11},{9,12},{10,... | collective-permute-start | bytes 98312 | tf_op jit(solution)/shard_map/ppermute | solution.py:24
  209.2 10.7 %collective-permute-start.25 = (bf16[32,512]{1,0:T(8,128)(2,1)}, bf16[32,512]{1,0:T(8,128)(2,1)S(1)}, u32[]{:S(2)}, u32[]{:S(2)}) collective-permute-start(bf16[32,512]{1,0:T(8,128)(2,1)} %get-tuple-element.117), channel_id=1, source_target_pairs={{0,4},{1,5},{2,6},{3,7},{4,0},{5,1},{6,2},{7,3},{8,12},{9,13},{10,... | collective-permute-start | bytes 98312 | tf_op jit(solution)/shard_map/ppermute | solution.py:24
  211.6 8.3 %collective-permute-start.26 = (bf16[32,512]{1,0:T(8,128)(2,1)}, bf16[32,512]{1,0:T(8,128)(2,1)S(1)}, u32[]{:S(2)}, u32[]{:S(2)}) collective-permute-start(bf16[32,512]{1,0:T(8,128)(2,1)} %get-tuple-element.118), channel_id=1, source_target_pairs={{0,5},{1,6},{2,7},{3,0},{4,1},{5,2},{6,3},{7,4},{8,13},{9,14},{10,... | collective-permute-start | bytes 98312 | tf_op jit(solution)/shard_map/ppermute | solution.py:24
  213.1 6.9 %collective-permute-start.27 = (bf16[32,512]{1,0:T(8,128)(2,1)}, bf16[32,512]{1,0:T(8,128)(2,1)S(1)}, u32[]{:S(2)}, u32[]{:S(2)}) collective-permute-start(bf16[32,512]{1,0:T(8,128)(2,1)} %get-tuple-element.119), channel_id=1, source_target_pairs={{0,6},{1,7},{2,0},{3,1},{4,2},{5,3},{6,4},{7,5},{8,14},{9,15},{10,... | collective-permute-start | bytes 98312 | tf_op jit(solution)/shard_map/ppermute | solution.py:24
  218.8 5.0 %collective-permute-start.28 = (bf16[32,512]{1,0:T(8,128)(2,1)}, bf16[32,512]{1,0:T(8,128)(2,1)S(1)}, u32[]{:S(2)}, u32[]{:S(2)}) collective-permute-start(bf16[32,512]{1,0:T(8,128)(2,1)} %get-tuple-element.120), channel_id=1, source_target_pairs={{0,7},{1,0},{2,1},{3,2},{4,3},{5,4},{6,5},{7,6},{8,15},{9,8},{10,9... | collective-permute-start | bytes 98312 | tf_op jit(solution)/shard_map/ppermute | solution.py:24
  (36 other events, 366.8 us)
where the time goes:
time: 233 us; the launch traced here: 232 us
  Pallas kernels  103 us (44%)
  starting transfers between devices  55 us (24%)
  waiting for transfers between devices  39.6 us (17%)
  local copies, waits for them, and re-layouts  19.4 us (8%)
  other arithmetic  13.5 us (6%)
    pallas_call x10, Pallas kernels, kernel_call(): pl.pallas_call(run, in_specs=[pl.BlockSpec(memory_space=pltpu.SMEM)] + [n...  80.2 us
    ppermute x15, waiting for transfers between devices, swapped(): return lax.ppermute(value, axis, [(i, i ^ by) for i in range(count)])  31 us
    ppermute x16, starting transfers between devices, from_behind(): return lax.ppermute(value, axis, pairs)  23.8 us
    pallas_call x1, Pallas kernels, ffn_part(): pl.pallas_call(lambda *refs: ffn_body(sums, not before, last, *refs), gri...  22.3 us
    ppermute x15, starting transfers between devices, swapped(): return lax.ppermute(value, axis, [(i, i ^ by) for i in range(count)])  11.9 us
    ppermute x16, waiting for transfers between devices, from_behind(): return lax.ppermute(value, axis, pairs)  8.59 us
    all_to_all x1, starting transfers between devices, split_form(): came = lax.all_to_all(sent, 'ctx', 0, 0, tiled=True)  7.15 us
    dynamic_slice x4, local copies, waits for them, and re-layouts, own_columns(): return lax.dynamic_slice_in_dim(weights, place * size, size, axis)  6.82 us
  transfers between devices with their start and end apart: 34, of which 9 were waited for; matrix products, arithmetic and copies ran while one was open for 11% of the time, Pallas kernels for 37%

commit v1 on v0

--- a/solution.py
+++ b/solution.py
@@ -637,7 +637,7 @@
         out_ref[:, at] = heads.T.astype(jnp.bfloat16)
         return carry
 
-    lax.fori_loop(0, chunks, one_head, 0)
+    lax.fori_loop(0, chunks, one_head, 0, unroll=2)
     for copy in leaving:
         copy.wait()
 
@@ -1307,7 +1307,7 @@
     def arrays_of(shards):
         return [shard.array if isinstance(shard, Part) else shard for shard in shards]
 
-    cot_ready = after(cot_own, *x_shards[-2:])
+    cot_ready = after(cot_own, *x_shards[-2:], early[0])
     cot_along = along(cot_ready)
     cot_across = across(cot_along[:1])
     attn_low = after(attn_low, *cot_along, *cot_across)
@@ -1342,10 +1342,11 @@
             weights,
         )
     ]
-    came = after(came, factors[0][0], *arrays_of(att_across[1:2]))
+    came = after(came, factors[0][0])
     low, head_gains = head_gradients(
         where, acts, w_head, q_row, k_row, freq, base, came, head_dim
     )
+    low = after(low, *arrays_of(att_across[1:2]))
     back = lax.all_to_all(low, "ctx", 0, 0, tiled=True)
     def core_sum(kept, given):
         total = kept.astype(jnp.float32) + swapped(given, "dp", 1).astype(jnp.float32)

time: 233 us -> 223 us (0.957)
  waiting for transfers between devices: 39.6 us -> 33.2 us
    ppermute x15, waiting for transfers between devices: 31 us -> 20.2 us  [swapped(): return lax.ppermute(value, axis, [(i, i ^ by) for i in range(count)])]
    ppermute x16, waiting for transfers between devices: 8.59 us -> 12.9 us  [from_behind(): return lax.ppermute(value, axis, pairs)]
  transfers between devices with their start and end apart: 34 -> 34, of which waited for: 9 -> 10; matrix products, arithmetic and copies ran while one was open for 11% -> 11% of each run, Pallas kernels for 37% -> 45%
where the time goes in v1:
time: 223 us; the launch traced here: 222 us
  Pallas kernels  102 us (46%)
  starting transfers between devices  53.5 us (24%)
  waiting for transfers between devices  33.2 us (15%)
  local copies, waits for them, and re-layouts  17.7 us (8%)
  other arithmetic  13.6 us (6%)
    pallas_call x10, Pallas kernels, kernel_call(): pl.pallas_call(run, in_specs=[pl.BlockSpec(memory_space=pltpu.SMEM)] + [n...  79.6 us
    ppermute x16, starting transfers between devices, from_behind(): return lax.ppermute(value, axis, pairs)  22.5 us
    pallas_call x1, Pallas kernels, ffn_part(): pl.pallas_call(lambda *refs: ffn_body(sums, not before, last, *refs), gri...  22.3 us
    ppermute x15, waiting for transfers between devices, swapped(): return lax.ppermute(value, axis, [(i, i ^ by) for i in range(count)])  20.2 us
    ppermute x16, waiting for transfers between devices, from_behind(): return lax.ppermute(value, axis, pairs)  12.9 us
    ppermute x15, starting transfers between devices, swapped(): return lax.ppermute(value, axis, [(i, i ^ by) for i in range(count)])  12.6 us
    dynamic_slice x4, local copies, waits for them, and re-layouts, own_columns(): return lax.dynamic_slice_in_dim(weights, place * size, size, axis)  6.82 us
    all_to_all x1, starting transfers between devices, split_form(): came = lax.all_to_all(sent, 'ctx', 0, 0, tiled=True)  6.26 us
  transfers between devices with their start and end apart: 34, of which 10 were waited for; matrix products, arithmetic and copies ran while one was open for 11% of the time, Pallas kernels for 45%

profile of v1, /device:TPU:18, one launch (start us, length us, event | category | flops | bytes accessed | tf_op | source)
XLA Modules:
  0.0 222.0 jit_solution(8827804329751401070)
XLA Ops:
  3.8 3.2 %constant_dynamic-slice_fusion.9 = (bf16[1024,576]{1,0:T(8,128)(2,1)S(1)}, bf16[1024,576]{1,0:T(8,128)(2,1)S(1)}) fusion(bf16[1024,4608]{1,0:T(8,128)(2,1)} %refs_7_.1, s32[]{:T(128)S(6)} %select_n.65, bf16[1024,4608]{1,0:T(8,128)(2,1)} %refs_6_.1), kind=kLoop, calls=%fused_computation.44 | loop fusion | bytes 4718596 | tf_op jit(solution)/shard_map/dynamic_slice | solution.py:1245
  7.1 1.7 fusion.2.refs_14_
  13.2 1.8 collective-permute-start.4
  15.6 3.1 %collective-permute-done.1.refs_0_.refs_2_ = bf16[128,1024]{1,0:T(8,128)(2,1)S(1)} collective-permute-done((bf16[128,1024]{1,0:T(8,128)(2,1)S(1)}, bf16[128,1024]{1,0:T(8,128)(2,1)S(1)}, u32[]{:S(2)}, u32[]{:S(2)}) %collective-permute-start.1) | collective-permute-done | bytes 262176 | tf_op jit(solution)/shard_map/ppermute | solution.py:24
  24.0 6.5 %key_value_part.2 = (bf16[8,128,1024]{2,1,0:T(8,128)(2,1)}, bf16[8,128,1024]{2,1,0:T(8,128)(2,1)}) custom-call(s32[4]{0:T(128)} %pad_add_fusion.1.scalars_ref, bf16[128,1024]{1,0:T(8,128)(2,1)} %bitcast.44, bf16[128,1024]{1,0:T(8,128)(2,1)} %copy-done.28, bf16[128,1024]{1,0:T(8,128)(2,1)} %copy-done.29, ...), custom_call_target="tpu_custom_call" | custom-call | flops 1073741824 | bytes 7476736 | tf_op jit(solution)/shard_map/key_value_part/pallas_call | solution.py:467
  31.7 4.8 %key_value_part.3 = (bf16[8,128,1024]{2,1,0:T(8,128)(2,1)}, bf16[8,128,1024]{2,1,0:T(8,128)(2,1)}) custom-call(s32[2]{0:T(128)} %pad_add_fusion.2.scalars_ref, bf16[128,1024]{1,0:T(8,128)(2,1)} %copy-done.10, bf16[128,1024]{1,0:T(8,128)(2,1)} %copy-done.11, bf16[1024,512]{1,0:T(8,128)(2,1)} %refs_14_.1, ...), custom_call_target="tpu_custom_call", output_to_operand_aliasing={{0}: (9, {}), {1}: (10, {})} | custom-call | flops 536870912 | bytes 6952448 | tf_op jit(solution)/shard_map/key_value_part/pallas_call | solution.py:467
  38.0 1.7 collective-permute-start.9
  39.8 4.0 %collective-permute-start.8 = (bf16[128,1024]{1,0:T(8,128)(2,1)S(1)}, bf16[128,1024]{1,0:T(8,128)(2,1)S(1)}, u32[]{:S(2)}, u32[]{:S(2)}) collective-permute-start(bf16[128,1024]{1,0:T(8,128)(2,1)S(1)} %bitcast.56), channel_id=1, source_target_pairs={{0,4},{1,5},{2,6},{3,7},{4,0},{5,1},{6,2},{7,3},{8,12},{9,13},{10,... | collective-permute-start | bytes 786440 | tf_op jit(solution)/shard_map/ppermute | solution.py:24
  45.6 13.0 %attend.1 = (bf16[128,1024]{1,0:T(8,128)(2,1)}, bf16[8,128,1024]{2,1,0:T(8,128)(2,1)}) custom-call(s32[10]{0:T(128)} %stack.120.scalars_ref, bf16[128,1024]{1,0:T(8,128)(2,1)} %copy-done.9, bf16[128,1024]{1,0:T(8,128)(2,1)} %copy-done.8, bf16[1024,512]{1,0:T(8,128)(2,1)} %refs_14_.1, bf16[1024,512]{1,0:T(8,128)(2,1)} %refs_15_.1, ...), custom_call_target="tpu_custom_call", output_to_operand_aliasing={{1}: (18, {})} | custom-call | flops 1342177280 | bytes 20060160 | tf_op jit(solution)/shard_map/attend/pallas_call | solution.py:467
  58.6 1.8 collective-permute-done.8.refs_10_
  60.5 2.7 %collective-permute-done.7.refs_9_ = bf16[128,1024]{1,0:T(8,128)(2,1)S(1)} collective-permute-done((bf16[128,1024]{1,0:T(8,128)(2,1)S(1)}, bf16[128,1024]{1,0:T(8,128)(2,1)S(1)}, u32[]{:S(2)}, u32[]{:S(2)}) %collective-permute-start.7) | collective-permute-done | bytes 262176 | tf_op jit(solution)/shard_map/ppermute | solution.py:24
  66.6 2.0 collective-permute-start.11
  68.7 22.3 %ffn_part.1 = (bf16[128,1024]{1,0:T(8,128)(2,1)}, f32[128,1024]{1,0:T(8,128)}, bf16[8,128,256]{2,1,0:T(8,128)(2,1)}, f32[1,1024]{1,0:T(1,128)}) custom-call(s32[2]{0:T(128)} %pad_add_fusion.refs_0_.scalars_ref, bf16[128,1024]{1,0:T(8,128)(2,1)} %bitcast.46, bf16[128,1024]{1,0:T(8,128)(2,1)} %get-tuple-element.80.refs_2_.refs_4_, bf16[128,1024]{1,0:T(8,128)(2,1)} %bitcast.52, ...), custom_call_target="tpu_custom_call" | custom-call | flops 7247757312 | bytes 28311552 | tf_op jit(solution)/shard_map/ffn_part/pallas_call | solution.py:779
  91.1 6.3 %all-to-all-start = ((bf16[8,128,256]{2,1,0:T(8,128)(2,1)}), bf16[8,128,256]{2,1,0:T(8,128)(2,1)S(1)}, u32[]{:S(2)}, u32[]{:S(2)}) async-start(bf16[8,128,256]{2,1,0:T(8,128)(2,1)} %get-tuple-element.87), calls=%async_computation | async-start | bytes 1048576 | tf_op jit(solution)/shard_map/all_to_all | solution.py:1334
  98.7 10.0 %factor_part.1 = (bf16[512,1024]{1,0:T(8,128)(2,1)}, bf16[512,1024]{1,0:T(8,128)(2,1)}, bf16[512,640]{1,0:T(8,128)(2,1)}, bf16[512,640]{1,0:T(8,128)(2,1)}, bf16[512,640]{1,0:T(8,128)(2,1)}) custom-call(s32[5]{0:T(128)} %stack.132.scalars_ref, bf16[128,1024]{1,0:T(8,128)(2,1)} %bitcast.47, bf16[128,1024]{1,0:T(8,128)(2,1)} %copy-done.29, ...), custom_call_target="tpu_custom_call" | custom-call | flops 3087007744 | bytes 13242368 | tf_op jit(solution)/shard_map/factor_part/pallas_call | solution.py:467
  109.6 14.8 %head_gradients.1 = (bf16[8,128,256]{2,1,0:T(8,128)(2,1)}, f32[8,128]{1,0:T(8,128)}) custom-call(s32[2]{0:T(128)} %pad_add_fusion.refs_0_.scalars_ref, bf16[1024,256]{1,0:T(8,128)(2,1)} %pad_maximum_fusion.2.refs_0_.refs_2_, f32[1,128]{1,0:T(1,128)} %maximum_bitcast_fusion.1.refs_10_.refs_1_, f32[1,128]{1,0:T(1,128)} %maximum_bitcast_fusion.refs_7_.refs_5_.refs_2_, ...), custom_call_target="tpu_custom_call" | custom-call | flops 1476395008 | bytes 3807232 | tf_op jit(solution)/shard_map/head_gradients/pallas_call | solution.py:467
  124.4 6.0 %all-to-all-start.1 = ((bf16[8,128,256]{2,1,0:T(8,128)(2,1)}), bf16[8,128,256]{2,1,0:T(8,128)(2,1)S(1)}, u32[]{:S(2)}, u32[]{:S(2)}) async-start(bf16[8,128,256]{2,1,0:T(8,128)(2,1)} %get-tuple-element.104.refs_0_), calls=%async_computation.1 | async-start | bytes 1048576 | tf_op jit(solution)/shard_map/all_to_all | solution.py:1350
  131.0 16.2 %last_products.1 = (bf16[512,1792]{1,0:T(8,128)(2,1)}, bf16[512,1792]{1,0:T(8,128)(2,1)}) custom-call(s32[6]{0:T(128)} %stack.137.scalars_ref, bf16[128,1024]{1,0:T(8,128)(2,1)} %copy-done.28, bf16[128,1024]{1,0:T(8,128)(2,1)} %collective-permute-done.4.refs_3_.refs_1_, bf16[128,1024]{1,0:T(8,128)(2,1)} %copy-done.11, bf16[128,1024]{1,0:T(8,128)(2,1)} %copy-done.8, ...), custom_call_target="tpu_custom_call" | custom-call | flops 6710886400 | bytes 16912384 | tf_op jit(solution)/shard_map/last_products/pallas_call | solution.py:467
  147.4 4.0 %collective-permute-done.17 = bf16[512,1792]{1,0:T(8,128)(2,1)S(1)} collective-permute-done((bf16[512,1792]{1,0:T(8,128)(2,1)}, bf16[512,1792]{1,0:T(8,128)(2,1)S(1)}, u32[]{:S(2)}, u32[]{:S(2)}) %collective-permute-start.17) | collective-permute-done | bytes 1835040 | tf_op jit(solution)/shard_map/ppermute | solution.py:1198
  151.3 1.9 add_convert_fusion
  153.4 1.6 collective-permute-start.18
  156.5 7.8 %head_products.1 = (f32[1024,1]{1,0:T(8,128)}, f32[128,1024]{1,0:T(8,128)}, bf16[512,256]{1,0:T(8,128)(2,1)}, bf16[512,256]{1,0:T(8,128)(2,1)}, bf16[64,1024]{1,0:T(8,128)(2,1)}, /*index=5*/bf16[64,1024]{1,0:T(8,128)(2,1)}) custom-call(s32[10]{0:T(128)} %stack.127.scalars_ref, bf16[8,128,256]{2,1,0:T(8,128)(2,1)} %get-tuple-element.104.refs_0_, ...), custom_call_target="tpu_custom_call" | custom-call | flops 1342177280 | bytes 12591104 | tf_op jit(solution)/shard_map/head_products/pallas_call | solution.py:467
  165.7 10.2 %collective-permute-done.18 = bf16[256,1792]{1,0:T(8,128)(2,1)S(1)} collective-permute-done((bf16[256,1792]{1,0:T(8,128)(2,1)S(1)}, bf16[256,1792]{1,0:T(8,128)(2,1)S(1)}, u32[]{:S(2)}, u32[]{:S(2)}) %collective-permute-start.18) | collective-permute-done | bytes 917536 | tf_op jit(solution)/shard_map/ppermute | solution.py:1198
  177.0 6.1 %all-to-all-start.2 = ((bf16[8,32,1792]{2,1,0:T(8,128)(2,1)}), bf16[8,32,1792]{2,1,0:T(8,128)(2,1)S(1)}, u32[]{:S(2)}, u32[]{:S(2)}) async-start(bf16[8,32,1792]{2,1,0:T(8,128)(2,1)} %bitcast.25), calls=%async_computation.2 | async-start | bytes 1835008 | tf_op jit(solution)/shard_map/all_to_all | solution.py:1388
  187.9 4.5 %collective-permute-done.21 = bf16[288,256]{1,0:T(8,128)(2,1)S(1)} collective-permute-done((bf16[288,256]{1,0:T(8,128)(2,1)S(1)}, bf16[288,256]{1,0:T(8,128)(2,1)S(1)}, u32[]{:S(2)}, u32[]{:S(2)}) %collective-permute-start.21) | collective-permute-done | bytes 147488 | tf_op jit(solution)/shard_map/ppermute | solution.py:1198
  193.7 1.8 cut_blocks.1
  197.1 2.0 collective-permute-start.24
  199.0 2.4 %collective-permute-start.25 = (bf16[32,512]{1,0:T(8,128)(2,1)}, bf16[32,512]{1,0:T(8,128)(2,1)S(1)}, u32[]{:S(2)}, u32[]{:S(2)}) collective-permute-start(bf16[32,512]{1,0:T(8,128)(2,1)} %get-tuple-element.119), channel_id=1, source_target_pairs={{0,4},{1,5},{2,6},{3,7},{4,0},{5,1},{6,2},{7,3},{8,12},{9,13},{10,... | collective-permute-start | bytes 98312 | tf_op jit(solution)/shard_map/ppermute | solution.py:24
  202.9 4.3 %collective-permute-start.27 = (bf16[32,512]{1,0:T(8,128)(2,1)}, bf16[32,512]{1,0:T(8,128)(2,1)S(1)}, u32[]{:S(2)}, u32[]{:S(2)}) collective-permute-start(bf16[32,512]{1,0:T(8,128)(2,1)} %get-tuple-element.121), channel_id=1, source_target_pairs={{0,6},{1,7},{2,0},{3,1},{4,2},{5,3},{6,4},{7,5},{8,14},{9,15},{10,... | collective-permute-start | bytes 98312 | tf_op jit(solution)/shard_map/ppermute | solution.py:24
  209.8 3.8 %collective-permute-done.28.refs_7_ = bf16[32,512]{1,0:T(8,128)(2,1)S(1)} collective-permute-done((bf16[32,512]{1,0:T(8,128)(2,1)}, bf16[32,512]{1,0:T(8,128)(2,1)S(1)}, u32[]{:S(2)}, u32[]{:S(2)}) %collective-permute-start.28) | collective-permute-done | bytes 32800 | tf_op jit(solution)/shard_map/ppermute | solution.py:24
  214.2 2.1 joined_out.1
  219.2 2.6 %spread_out.1 = (f32[32,4608]{1,0:T(8,128)}, f32[32,4608]{1,0:T(8,128)}, f32[32,4608]{1,0:T(8,128)}) custom-call(s32[1]{0:T(128)} %bitcast.scalars_ref, bf16[8,32,1792]{2,1,0:T(8,128)(2,1)} %copy-done.1), custom_call_target="tpu_custom_call" | custom-call | bytes 2686976 | tf_op jit(solution)/shard_map/spread_out/pallas_call | solution.py:467
  (167 shorter events, 42.8 us)
Async XLA Ops:
  0.6 22.6 %collective-permute-start.3 = (bf16[128,1024]{1,0:T(8,128)(2,1)}, bf16[128,1024]{1,0:T(8,128)(2,1)S(1)}, u32[]{:S(2)}, u32[]{:S(2)}) collective-permute-start(bf16[128,1024]{1,0:T(8,128)(2,1)} %bitcast.42), channel_id=1, source_target_pairs={{0,1},{1,0},{2,3},{3,2},{4,5},{5,4},{6,7},{7,6},{8,9},{9,8},{10,11... | collective-permute-start | bytes 786440 | tf_op jit(solution)/shard_map/ppermute | solution.py:1198
  1.2 9.9 %collective-permute-start = (bf16[128,1024]{1,0:T(8,128)(2,1)}, bf16[128,1024]{1,0:T(8,128)(2,1)S(1)}, u32[]{:S(2)}, u32[]{:S(2)}) collective-permute-start(bf16[128,1024]{1,0:T(8,128)(2,1)} %bitcast.43), channel_id=1, source_target_pairs={{0,2},{1,3},{2,4},{3,5},{4,6},{5,7},{6,0},{7,1},{8,10},{9,11},{10,... | collective-permute-start | bytes 786440 | tf_op jit(solution)/shard_map/ppermute | solution.py:24
  11.2 7.5 %collective-permute-start.1 = (bf16[128,1024]{1,0:T(8,128)(2,1)S(1)}, bf16[128,1024]{1,0:T(8,128)(2,1)S(1)}, u32[]{:S(2)}, u32[]{:S(2)}) collective-permute-start(bf16[128,1024]{1,0:T(8,128)(2,1)S(1)} %collective-permute-done.refs_2_.refs_1_), channel_id=1, source_target_pairs={{0,2},{1,3},{2,4},{3,5},{4,6},{5,7},{6,0},{7,1},{8,10},{9,11},{10,... | collective-permute-start | bytes 786440 | tf_op jit(solution)/shard_map/ppermute | solution.py:24
  13.2 10.1 %collective-permute-start.4 = (bf16[128,1024]{1,0:T(8,128)(2,1)S(1)}, bf16[128,1024]{1,0:T(8,128)(2,1)}, u32[]{:S(2)}, u32[]{:S(2)}) collective-permute-start(bf16[128,1024]{1,0:T(8,128)(2,1)S(1)} %collective-permute-done.refs_2_.refs_1_), channel_id=1, source_target_pairs={{0,1},{1,0},{2,3},{3,2},{4,5},{5,4},{6,7},{7,6},{8,9},{9,8},{10,11... | collective-permute-start | bytes 786440 | tf_op jit(solution)/shard_map/ppermute | solution.py:1198
  18.7 11.7 %collective-permute-start.5 = (bf16[128,1024]{1,0:T(8,128)(2,1)S(1)}, bf16[128,1024]{1,0:T(8,128)(2,1)S(1)}, u32[]{:S(2)}, u32[]{:S(2)}) collective-permute-start(bf16[128,1024]{1,0:T(8,128)(2,1)S(1)} %collective-permute-done.1.refs_0_.refs_2_), channel_id=1, source_target_pairs={{0,1},{1,0},{2,3},{3,2},{4,5},{5,4},{6,7},{7,6},{8,9},{9,8},{10,11... | collective-permute-start | bytes 786440 | tf_op jit(solution)/shard_map/ppermute | solution.py:1198
  20.2 10.3 %collective-permute-start.2 = (bf16[128,1024]{1,0:T(8,128)(2,1)S(1)}, bf16[128,1024]{1,0:T(8,128)(2,1)S(1)}, u32[]{:S(2)}, u32[]{:S(2)}) collective-permute-start(bf16[128,1024]{1,0:T(8,128)(2,1)S(1)} %collective-permute-done.1.refs_0_.refs_2_), channel_id=1, source_target_pairs={{0,2},{1,3},{2,4},{3,5},{4,6},{5,7},{6,0},{7,1},{8,10},{9,11},{10,... | collective-permute-start | bytes 786440 | tf_op jit(solution)/shard_map/ppermute | solution.py:24
  30.5 6.4 %collective-permute-start.6 = (bf16[128,1024]{1,0:T(8,128)(2,1)S(1)}, bf16[128,1024]{1,0:T(8,128)(2,1)S(1)}, u32[]{:S(2)}, u32[]{:S(2)}) collective-permute-start(bf16[128,1024]{1,0:T(8,128)(2,1)S(1)} %collective-permute-done.2.refs_0_.refs_3_), channel_id=1, source_target_pairs={{0,1},{1,0},{2,3},{3,2},{4,5},{5,4},{6,7},{7,6},{8,9},{9,8},{10,11... | collective-permute-start | bytes 786440 | tf_op jit(solution)/shard_map/ppermute | solution.py:1198
  36.9 21.7 %collective-permute-start.10 = (bf16[128,1024]{1,0:T(8,128)(2,1)S(1)}, bf16[128,1024]{1,0:T(8,128)(2,1)S(1)}, u32[]{:S(2)}, u32[]{:S(2)}) collective-permute-start(bf16[128,1024]{1,0:T(8,128)(2,1)S(1)} %bitcast.54), channel_id=1, source_target_pairs={{0,1},{1,0},{2,3},{3,2},{4,5},{5,4},{6,7},{7,6},{8,9},{9,8},{10,11... | collective-permute-start | bytes 786440 | tf_op jit(solution)/shard_map/ppermute | solution.py:1198
  38.0 20.6 %collective-permute-start.9 = (bf16[128,1024]{1,0:T(8,128)(2,1)S(1)}, bf16[128,1024]{1,0:T(8,128)(2,1)S(1)}, u32[]{:S(2)}, u32[]{:S(2)}) collective-permute-start(bf16[128,1024]{1,0:T(8,128)(2,1)S(1)} %bitcast.55), channel_id=1, source_target_pairs={{0,6},{1,7},{2,0},{3,1},{4,2},{5,3},{6,4},{7,5},{8,14},{9,15},{10,... | collective-permute-start | bytes 786440 | tf_op jit(solution)/shard_map/ppermute | solution.py:24
  39.8 20.7 %collective-permute-start.8 = (bf16[128,1024]{1,0:T(8,128)(2,1)S(1)}, bf16[128,1024]{1,0:T(8,128)(2,1)S(1)}, u32[]{:S(2)}, u32[]{:S(2)}) collective-permute-start(bf16[128,1024]{1,0:T(8,128)(2,1)S(1)} %bitcast.56), channel_id=1, source_target_pairs={{0,4},{1,5},{2,6},{3,7},{4,0},{5,1},{6,2},{7,3},{8,12},{9,13},{10,... | collective-permute-start | bytes 786440 | tf_op jit(solution)/shard_map/ppermute | solution.py:24
  43.8 19.5 %collective-permute-start.7 = (bf16[128,1024]{1,0:T(8,128)(2,1)S(1)}, bf16[128,1024]{1,0:T(8,128)(2,1)S(1)}, u32[]{:S(2)}, u32[]{:S(2)}) collective-permute-start(bf16[128,1024]{1,0:T(8,128)(2,1)S(1)} %bitcast.57), channel_id=1, source_target_pairs={{0,2},{1,3},{2,4},{3,5},{4,6},{5,7},{6,0},{7,1},{8,10},{9,11},{10,... | collective-permute-start | bytes 786440 | tf_op jit(solution)/shard_map/ppermute | solution.py:24
  63.3 27.8 %collective-permute-start.15 = (bf16[3,128,1024]{2,1,0:T(8,128)(2,1)S(1)}, bf16[3,128,1024]{2,1,0:T(8,128)(2,1)}, u32[]{:S(2)}, u32[]{:S(2)}) collective-permute-start(bf16[3,128,1024]{2,1,0:T(8,128)(2,1)S(1)} %pad_maximum_fusion), channel_id=1, source_target_pairs={{0,1},{1,0},{2,3},{3,2},{4,5},{5,4},{6,7},{7,6},{8,9},{9,8},{10,11... | collective-permute-start | bytes 2359304 | tf_op jit(solution)/shard_map/ppermute | solution.py:1198
  64.5 26.6 %collective-permute-start.14 = (bf16[128,1024]{1,0:T(8,128)(2,1)}, bf16[128,1024]{1,0:T(8,128)(2,1)S(1)}, u32[]{:S(2)}, u32[]{:S(2)}) collective-permute-start(bf16[128,1024]{1,0:T(8,128)(2,1)} %get-tuple-element.80.refs_2_.refs_4_), channel_id=1, source_target_pairs={{0,1},{1,0},{2,3},{3,2},{4,5},{5,4},{6,7},{7,6},{8,9},{9,8},{10,11... | collective-permute-start | bytes 786440 | tf_op jit(solution)/shard_map/ppermute | solution.py:1198
  66.0 25.1 %collective-permute-start.13 = (bf16[128,1024]{1,0:T(8,128)(2,1)}, bf16[128,1024]{1,0:T(8,128)(2,1)S(1)}, u32[]{:S(2)}, u32[]{:S(2)}) collective-permute-start(bf16[128,1024]{1,0:T(8,128)(2,1)} %get-tuple-element.80.refs_2_.refs_4_), channel_id=1, source_target_pairs={{0,6},{1,7},{2,0},{3,1},{4,2},{5,3},{6,4},{7,5},{8,14},{9,15},{10,... | collective-permute-start | bytes 786440 | tf_op jit(solution)/shard_map/ppermute | solution.py:24
  66.0 25.1 %collective-permute-start.12 = (bf16[128,1024]{1,0:T(8,128)(2,1)}, bf16[128,1024]{1,0:T(8,128)(2,1)S(1)}, u32[]{:S(2)}, u32[]{:S(2)}) collective-permute-start(bf16[128,1024]{1,0:T(8,128)(2,1)} %get-tuple-element.80.refs_2_.refs_4_), channel_id=1, source_target_pairs={{0,4},{1,5},{2,6},{3,7},{4,0},{5,1},{6,2},{7,3},{8,12},{9,13},{10,... | collective-permute-start | bytes 786440 | tf_op jit(solution)/shard_map/ppermute | solution.py:24
  66.6 24.5 %collective-permute-start.11 = (bf16[128,1024]{1,0:T(8,128)(2,1)}, bf16[128,1024]{1,0:T(8,128)(2,1)S(1)}, u32[]{:S(2)}, u32[]{:S(2)}) collective-permute-start(bf16[128,1024]{1,0:T(8,128)(2,1)} %get-tuple-element.80.refs_2_.refs_4_), channel_id=1, source_target_pairs={{0,2},{1,3},{2,4},{3,5},{4,6},{5,7},{6,0},{7,1},{8,10},{9,11},{10,... | collective-permute-start | bytes 786440 | tf_op jit(solution)/shard_map/ppermute | solution.py:24
  91.1 17.6 %all-to-all-start = ((bf16[8,128,256]{2,1,0:T(8,128)(2,1)}), bf16[8,128,256]{2,1,0:T(8,128)(2,1)S(1)}, u32[]{:S(2)}, u32[]{:S(2)}) async-start(bf16[8,128,256]{2,1,0:T(8,128)(2,1)} %get-tuple-element.87), calls=%async_computation | async-start | bytes 1048576 | tf_op jit(solution)/shard_map/all_to_all | solution.py:1334
  97.5 26.9 %collective-permute-start.16 = (bf16[3,128,1024]{2,1,0:T(8,128)(2,1)S(1)}, bf16[3,128,1024]{2,1,0:T(8,128)(2,1)S(1)}, u32[]{:S(2)}, u32[]{:S(2)}) collective-permute-start(bf16[3,128,1024]{2,1,0:T(8,128)(2,1)S(1)} %pad_maximum_fusion.1), channel_id=1, source_target_pairs={{0,1},{1,0},{2,3},{3,2},{4,5},{5,4},{6,7},{7,6},{8,9},{9,8},{10,11... | collective-permute-start | bytes 2359304 | tf_op jit(solution)/shard_map/ppermute | solution.py:1198
  124.4 22.8 %all-to-all-start.1 = ((bf16[8,128,256]{2,1,0:T(8,128)(2,1)}), bf16[8,128,256]{2,1,0:T(8,128)(2,1)S(1)}, u32[]{:S(2)}, u32[]{:S(2)}) async-start(bf16[8,128,256]{2,1,0:T(8,128)(2,1)} %get-tuple-element.104.refs_0_), calls=%async_computation.1 | async-start | bytes 1048576 | tf_op jit(solution)/shard_map/all_to_all | solution.py:1350
  153.4 22.5 %collective-permute-start.18 = (bf16[256,1792]{1,0:T(8,128)(2,1)S(1)}, bf16[256,1792]{1,0:T(8,128)(2,1)S(1)}, u32[]{:S(2)}, u32[]{:S(2)}) collective-permute-start(bf16[256,1792]{1,0:T(8,128)(2,1)S(1)} %get-tuple-element.136), channel_id=1, source_target_pairs={{0,16},{8,24},{16,0},{24,8},{1,17},{9,25},{17,1},{25,9},{2,18},{10... | collective-permute-start | bytes 2752520 | tf_op jit(solution)/shard_map/ppermute | solution.py:1198
  177.0 6.7 %collective-permute-start.20 = (f32[2176]{0:T(1024)S(1)}, f32[2176]{0:T(1024)S(1)}, u32[]{:S(2)}, u32[]{:S(2)}) collective-permute-start(f32[2176]{0:T(1024)S(1)} %concatenate.34), channel_id=1, source_target_pairs={{0,8},{8,0},{16,24},{24,16},{1,9},{9,1},{17,25},{25,17},{2,10},{10... | collective-permute-start | bytes 26120 | tf_op jit(solution)/shard_map/ppermute | solution.py:1198
  177.0 41.3 %all-to-all-start.2 = ((bf16[8,32,1792]{2,1,0:T(8,128)(2,1)}), bf16[8,32,1792]{2,1,0:T(8,128)(2,1)S(1)}, u32[]{:S(2)}, u32[]{:S(2)}) async-start(bf16[8,32,1792]{2,1,0:T(8,128)(2,1)} %bitcast.25), calls=%async_computation.2 | async-start | bytes 1835008 | tf_op jit(solution)/shard_map/all_to_all | solution.py:1388
  183.2 4.1 %collective-permute-start.29 = (bf16[64,1024]{1,0:T(8,128)(2,1)}, bf16[64,1024]{1,0:T(8,128)(2,1)S(1)}, u32[]{:S(2)}, u32[]{:S(2)}) collective-permute-start(bf16[64,1024]{1,0:T(8,128)(2,1)} %get-tuple-element.129), channel_id=1, source_target_pairs={{0,8},{8,0},{16,24},{24,16},{1,9},{9,1},{17,25},{25,17},{2,10},{10... | collective-permute-start | bytes 393224 | tf_op jit(solution)/shard_map/ppermute | solution.py:1198
  185.6 6.7 %collective-permute-start.21 = (bf16[288,256]{1,0:T(8,128)(2,1)S(1)}, bf16[288,256]{1,0:T(8,128)(2,1)S(1)}, u32[]{:S(2)}, u32[]{:S(2)}) collective-permute-start(bf16[288,256]{1,0:T(8,128)(2,1)S(1)} %pad_maximum_fusion.3), channel_id=1, source_target_pairs={{0,16},{8,24},{16,0},{24,8},{1,17},{9,25},{17,1},{25,9},{2,18},{10... | collective-permute-start | bytes 442376 | tf_op jit(solution)/shard_map/ppermute | solution.py:1198
  187.3 14.1 %collective-permute-start.30 = (bf16[32,1024]{1,0:T(8,128)(2,1)S(1)}, bf16[32,1024]{1,0:T(8,128)(2,1)S(1)}, u32[]{:S(2)}, u32[]{:S(2)}) collective-permute-start(bf16[32,1024]{1,0:T(8,128)(2,1)S(1)} %constant_dynamic-slice_fusion), channel_id=1, source_target_pairs={{0,16},{8,24},{16,0},{24,8},{1,17},{9,25},{17,1},{25,9},{2,18},{10... | collective-permute-start | bytes 196616 | tf_op jit(solution)/shard_map/ppermute | solution.py:1198
  195.5 7.4 %collective-permute-start.22 = (bf16[32,512]{1,0:T(8,128)(2,1)}, bf16[32,512]{1,0:T(8,128)(2,1)S(1)}, u32[]{:S(2)}, u32[]{:S(2)}) collective-permute-start(bf16[32,512]{1,0:T(8,128)(2,1)} %get-tuple-element.116), channel_id=1, source_target_pairs={{0,1},{1,2},{2,3},{3,4},{4,5},{5,6},{6,7},{7,0},{8,9},{9,10},{10,1... | collective-permute-start | bytes 98312 | tf_op jit(solution)/shard_map/ppermute | solution.py:24
  197.0 11.6 %collective-permute-start.23 = (bf16[32,512]{1,0:T(8,128)(2,1)}, bf16[32,512]{1,0:T(8,128)(2,1)S(1)}, u32[]{:S(2)}, u32[]{:S(2)}) collective-permute-start(bf16[32,512]{1,0:T(8,128)(2,1)} %get-tuple-element.117), channel_id=1, source_target_pairs={{0,2},{1,3},{2,4},{3,5},{4,6},{5,7},{6,0},{7,1},{8,10},{9,11},{10,... | collective-permute-start | bytes 98312 | tf_op jit(solution)/shard_map/ppermute | solution.py:24
  197.1 12.6 %collective-permute-start.24 = (bf16[32,512]{1,0:T(8,128)(2,1)}, bf16[32,512]{1,0:T(8,128)(2,1)S(1)}, u32[]{:S(2)}, u32[]{:S(2)}) collective-permute-start(bf16[32,512]{1,0:T(8,128)(2,1)} %get-tuple-element.118), channel_id=1, source_target_pairs={{0,3},{1,4},{2,5},{3,6},{4,7},{5,0},{6,1},{7,2},{8,11},{9,12},{10,... | collective-permute-start | bytes 98312 | tf_op jit(solution)/shard_map/ppermute | solution.py:24
  199.0 10.7 %collective-permute-start.25 = (bf16[32,512]{1,0:T(8,128)(2,1)}, bf16[32,512]{1,0:T(8,128)(2,1)S(1)}, u32[]{:S(2)}, u32[]{:S(2)}) collective-permute-start(bf16[32,512]{1,0:T(8,128)(2,1)} %get-tuple-element.119), channel_id=1, source_target_pairs={{0,4},{1,5},{2,6},{3,7},{4,0},{5,1},{6,2},{7,3},{8,12},{9,13},{10,... | collective-permute-start | bytes 98312 | tf_op jit(solution)/shard_map/ppermute | solution.py:24
  201.4 8.3 %collective-permute-start.26 = (bf16[32,512]{1,0:T(8,128)(2,1)}, bf16[32,512]{1,0:T(8,128)(2,1)S(1)}, u32[]{:S(2)}, u32[]{:S(2)}) collective-permute-start(bf16[32,512]{1,0:T(8,128)(2,1)} %get-tuple-element.120), channel_id=1, source_target_pairs={{0,5},{1,6},{2,7},{3,0},{4,1},{5,2},{6,3},{7,4},{8,13},{9,14},{10,... | collective-permute-start | bytes 98312 | tf_op jit(solution)/shard_map/ppermute | solution.py:24
  202.9 6.9 %collective-permute-start.27 = (bf16[32,512]{1,0:T(8,128)(2,1)}, bf16[32,512]{1,0:T(8,128)(2,1)S(1)}, u32[]{:S(2)}, u32[]{:S(2)}) collective-permute-start(bf16[32,512]{1,0:T(8,128)(2,1)} %get-tuple-element.121), channel_id=1, source_target_pairs={{0,6},{1,7},{2,0},{3,1},{4,2},{5,3},{6,4},{7,5},{8,14},{9,15},{10,... | collective-permute-start | bytes 98312 | tf_op jit(solution)/shard_map/ppermute | solution.py:24
  208.6 5.0 %collective-permute-start.28 = (bf16[32,512]{1,0:T(8,128)(2,1)}, bf16[32,512]{1,0:T(8,128)(2,1)S(1)}, u32[]{:S(2)}, u32[]{:S(2)}) collective-permute-start(bf16[32,512]{1,0:T(8,128)(2,1)} %get-tuple-element.122), channel_id=1, source_target_pairs={{0,7},{1,0},{2,1},{3,2},{4,3},{5,4},{6,5},{7,6},{8,15},{9,8},{10,9... | collective-permute-start | bytes 98312 | tf_op jit(solution)/shard_map/ppermute | solution.py:24
  (36 other events, 349.1 us)
